TPU v7x, 256 devices: a whole 4x4x8 slice. The times are simulated.
256 devices in a mesh: leaf: 64 (over z, x, core), rhs: 4 (over y).
Axes of the slice: x: 4, y: 4, z: 8, core: 2. Of those that a mesh axis runs over, the one named last changes fastest.
Arguments:
- points: bfloat16 [131072, 784], P('leaf'), may hold values from -8 to 8
- vectors: bfloat16 [131072, 128], P('leaf', 'rhs'), may hold values from -6 to 6
- bases: float32 [512, 256, 64], P('leaf'), may hold values from -0.375 to 0.375
- leaf_coupling: float32 [512, 8, 64, 64], P('leaf'), may hold values from -0.75 to 0.75
- transfer: float32 [512, 64, 64], P('leaf'), may hold values from -0.75 to 0.75
- up_coupling: float32 [256, 8, 64, 64], P('leaf'), may hold values from -0.75 to 0.75
- far_leaf: int32 [512, 8], P('leaf'), may hold values from 0 to 511, as said below
- far_up: int32 [256, 8], P('leaf'), may hold values from 0 to 255, as said below
- near_lists: int32 [512, 8], P('leaf'), may hold values from -1 to 511, as said below
Outputs:
- product: float32 [131072, 128], P('leaf', 'rhs')
Inputs may be any that keep to these rules, and one draw needn't show every extreme that they name: `near_lists`: row i begins with i itself; the other entries are distinct leaves j with 0 < |i - j| <= 8, or -1 for an unused slot. `far_leaf`: each row holds 8 distinct leaves, each more than 8 away from the row's own leaf in index. `far_up`: each row holds 8 distinct parents, each at least 2 away from the row's own parent in index.
All inputs are finite; a program needn't handle non-finite values.
Results may differ from a plain program's by a relative error of at most 0.0025.
Values may be sent and summed in bfloat16 or wider, within the bound.
A program may use at most 128 MiB of HBM per device.

v0:
```python
from functools import partial

import jax
import jax.numpy as jnp
from jax import lax
from jax.sharding import PartitionSpec as P

HIGHEST = lax.Precision.HIGHEST
RIDGE = 0.5


def with_halo(block, sides, width):
    for axis, dim in sides:
        count = lax.axis_size(axis)
        forward = [(i, i + 1) for i in range(count - 1)]
        backward = [(target, source) for source, target in forward]
        low = lax.ppermute(
            lax.slice_in_dim(block, block.shape[dim] - width, None, axis=dim), axis, forward
        )
        high = lax.ppermute(lax.slice_in_dim(block, 0, width, axis=dim), axis, backward)
        block = jnp.concatenate([low, block, high], axis=dim)
    return block


def fold_rows(targets, piece):
    piece_rows = piece.shape[0]
    global_rows = lax.iota(jnp.int32, piece_rows)
    select = (targets[:, None] == global_rows[None, :]).astype(jnp.float32)
    return jnp.dot(select, piece, precision=HIGHEST, preferred_element_type=jnp.float32)


def local(
    points, vectors, bases, leaf_coupling, transfer, up_coupling, far_leaf, far_up, near_lists
):
    leaf_count = bases.shape[0]
    leaf_pts = bases.shape[1]
    rank_size = bases.shape[2]
    columns = vectors.shape[1]
    shard_rows = points.shape[0]
    features = points.shape[1]
    far_count = far_leaf.shape[1]
    far_upper = far_up.shape[1]
    half_count = leaf_count // 2
    device = lax.axis_index("leaf")
    vec_float = vectors.astype(jnp.float32).reshape(leaf_count, leaf_pts, columns)
    coeffs = jnp.einsum("lpr,lpc->lrc", bases, vec_float, precision=HIGHEST)
    lifted = jnp.einsum("lba,lbc->lac", transfer, coeffs, precision=HIGHEST)
    parents = lifted.reshape(half_count, 2, rank_size, columns).sum(axis=1)
    leaf_targets = far_leaf.reshape(-1)
    gathered = fold_rows(
        leaf_targets,
        lax.all_gather(coeffs.reshape(leaf_count, rank_size * columns), "leaf", axis=0, tiled=True),
    )
    leaf_field = jnp.einsum(
        "lkab,lkbc->lac",
        leaf_coupling,
        gathered.reshape(leaf_count, far_count, rank_size, columns),
        precision=HIGHEST,
    )
    up_targets = far_up.reshape(-1)
    up_gathered = fold_rows(
        up_targets,
        lax.all_gather(
            parents.reshape(half_count, rank_size * columns), "leaf", axis=0, tiled=True
        ),
    )
    upper_field = jnp.einsum(
        "qkab,qkbc->qac",
        up_coupling,
        up_gathered.reshape(half_count, far_upper, rank_size, columns),
        precision=HIGHEST,
    )
    pushed = jnp.einsum(
        "lab,lbc->lac", transfer, jnp.repeat(upper_field, 2, axis=0), precision=HIGHEST
    )
    far_part = jnp.einsum("lpr,lrc->lpc", bases, leaf_field + pushed, precision=HIGHEST).reshape(
        shard_rows, columns
    )
    window_points = with_halo(points, (("leaf", 0),), shard_rows)
    window_vectors = with_halo(vectors, (("leaf", 0),), shard_rows)
    dims_rowwise = (((1,), (1,)), ((0,), (0,)))
    window_sums = lax.dot_general(
        window_points, window_points, dims_rowwise, preferred_element_type=jnp.float32
    )
    own_sums = lax.dot_general(points, points, dims_rowwise, preferred_element_type=jnp.float32)
    first_leaf = device * leaf_count - leaf_count
    usable = near_lists >= 0
    window_leaf = jnp.where(usable, near_lists - first_leaf, 0)

    def near_tiles(vector_source, operands):
        own_points, own_norms, slot_ids, slot_usable = operands
        running = jnp.zeros((leaf_pts, vector_source.shape[1]), jnp.float32)
        for slot_index in range(slot_ids.shape[0]):
            begin_row = slot_ids[slot_index] * leaf_pts
            near_points = lax.dynamic_slice_in_dim(window_points, begin_row, leaf_pts, 0)
            near_norms = lax.dynamic_slice_in_dim(window_sums, begin_row, leaf_pts, 0)
            cross_terms = lax.dot_general(
                own_points,
                near_points,
                (((1,), (1,)), ((), ())),
                preferred_element_type=jnp.float32,
            )
            distance = own_norms[:, None] + near_norms[None, :] - 2.0 * cross_terms
            weight_mask = slot_usable[slot_index].astype(jnp.float32)
            kernel = (jnp.exp(-distance / features) * weight_mask).astype(jnp.bfloat16)
            near_vectors = lax.dynamic_slice_in_dim(vector_source, begin_row, leaf_pts, 0)
            running = running + jnp.dot(kernel, near_vectors, preferred_element_type=jnp.float32)
        return running

    point_blocks = points.reshape(leaf_count, leaf_pts, features)
    norm_blocks = own_sums.reshape(leaf_count, leaf_pts)
    near_part = lax.map(
        partial(near_tiles, window_vectors), (point_blocks, norm_blocks, window_leaf, usable)
    ).reshape(shard_rows, columns)
    return near_part + far_part + RIDGE * vectors.astype(jnp.float32)


def solution(mesh):
    return jax.shard_map(
        local,
        mesh=mesh,
        in_specs=(
            P("leaf", None),
            P("leaf", "rhs"),
            P("leaf", None, None),
            P("leaf", None, None, None),
            P("leaf", None, None),
            P("leaf", None, None, None),
            P("leaf", None),
            P("leaf", None),
            P("leaf", None),
        ),
        out_specs=P("leaf", "rhs"),
        check_vma=False,
    )
```

profile of v0, /device:TPU:127, one launch (start us, length us, event | category | flops | bytes accessed | tf_op | source)
XLA Modules:
  0.0 325.7 jit_solution(5154786369688142895)
XLA Ops:
  10.3 5.2 %collective-permute-start = (bf16[2048,784]{0,1:T(8,128)(2,1)}, bf16[2048,784]{0,1:T(8,128)(2,1)}, u32[]{:S(2)}, u32[]{:S(2)}) collective-permute-start(bf16[2048,784]{0,1:T(8,128)(2,1)} %param.11), channel_id=1, source_target_pairs={{0,4},{4,8},{8,12},{12,16},{16,20},{20,24},{24,28},{28,32},{32,36}... | collective-permute-start | bytes 9633800 | tf_op jit(solution)/shard_map/ppermute | solution.py:17
  15.6 1.9 collective-permute-start.1
  17.5 7.0 %collective-permute-start.2 = (bf16[2048,32]{0,1:T(8,128)(2,1)}, bf16[2048,32]{0,1:T(8,128)(2,1)S(1)}, u32[]{:S(2)}, u32[]{:S(2)}) collective-permute-start(bf16[2048,32]{0,1:T(8,128)(2,1)} %param.12), channel_id=1, source_target_pairs={{0,4},{4,8},{8,12},{12,16},{16,20},{20,24},{24,28},{28,32},{32,36}... | collective-permute-start | bytes 393224 | tf_op jit(solution)/shard_map/ppermute | solution.py:17
  24.5 1.9 collective-permute-start.3
  27.4 6.0 %copy.32 = bf16[2048,784]{1,0:T(8,128)(2,1)} copy(bf16[2048,784]{0,1:T(8,128)(2,1)} %param.11) | data formatting | bytes 6422528 | tf_op args[0]
  33.4 2.6 fusion.202
  36.1 17.3 %collective-permute-done.2 = bf16[2048,32]{0,1:T(8,128)(2,1)S(1)} collective-permute-done((bf16[2048,32]{0,1:T(8,128)(2,1)}, bf16[2048,32]{0,1:T(8,128)(2,1)S(1)}, u32[]{:S(2)}, u32[]{:S(2)}) %collective-permute-start.2) | collective-permute-done | bytes 131104 | tf_op jit(solution)/shard_map/ppermute | solution.py:17
  53.4 7.6 %collective-permute-done.3 = bf16[2048,32]{0,1:T(8,128)(2,1)S(1)} collective-permute-done((bf16[2048,32]{0,1:T(8,128)(2,1)}, bf16[2048,32]{0,1:T(8,128)(2,1)S(1)}, u32[]{:S(2)}, u32[]{:S(2)}) %collective-permute-start.3) | collective-permute-done | bytes 131104 | tf_op jit(solution)/shard_map/ppermute | solution.py:20
  62.6 4.1 %constant_dynamic-update-slice_fusion.2 = bf16[6144,784]{0,1:T(8,128)(2,1)} fusion(bf16[2048,784]{0,1:T(8,128)(2,1)} %collective-permute-done), kind=kLoop, calls=%fused_computation.203 | loop fusion | bytes 6422528
  66.7 1.9 constant_dynamic-update-slice_fusion.1
  68.6 4.0 %constant_dynamic-update-slice_fusion = bf16[6144,784]{0,1:T(8,128)(2,1)} fusion(bf16[6144,784]{0,1:T(8,128)(2,1)} %constant_dynamic-update-slice_fusion.1, bf16[2048,784]{0,1:T(8,128)(2,1)} %collective-permute-done.1), kind=kLoop, calls=%fused_computation.201 | loop fusion | bytes 6422528 | tf_op jit(solution)/shard_map/concatenate | solution.py:21
  72.6 13.5 %copy.33 = bf16[6144,784]{1,0:T(8,128)(2,1)} copy(bf16[6144,784]{0,1:T(8,128)(2,1)} %constant_dynamic-update-slice_fusion) | data formatting | bytes 19267584 | tf_op jit(solution)/shard_map/while | solution.py:112
  86.1 5.8 %fusion.201 = f32[6144]{0:T(1024)S(1)} fusion(bf16[6144,784]{0,1:T(8,128)(2,1)} %constant_dynamic-update-slice_fusion), kind=kLoop, calls=%fused_computation.181 | loop fusion | flops 14444544 | bytes 9658368 | tf_op jit(solution)/shard_map/dot_general | solution.py:82
  91.9 204.7 %while.10 = (s32[]{:T(128)}, f32[8,256,32]{1,2,0:T(8,128)}, f32[8,256]{1,0:T(8,128)S(1)}, s32[8,8]{1,0:T(8,128)S(1)}, f32[6144]{0:T(1024)S(1)}, /*index=5*/bf16[...) while((s32[]{:T(128)}, f32[8,256,32]{1,2,0:T(8,128)}, ...), condition=%wide.region_1.2_spmd, body=%wide.region_0.0_spmd.sunk | while | flops 859365376 | bytes 8408289 | solution.py:112
  99.2 1.6 fusion.288
  101.5 1.6 fusion.289
  103.9 1.6 fusion.290
  106.1 1.6 fusion.291
  110.6 1.6 fusion.293
  113.0 1.6 fusion.294
  115.2 2.3 fusion.295
  127.1 1.6 fusion.289
  131.7 1.6 fusion.291
  136.2 1.6 fusion.293
  138.5 1.8 fusion.294
  141.0 2.3 fusion.295
  152.8 1.6 fusion.289
  155.2 1.7 fusion.290
  157.5 1.6 fusion.291
  162.0 1.6 fusion.293
  164.3 1.6 fusion.294
  166.6 2.3 fusion.295
  178.4 1.6 fusion.289
  180.8 1.6 fusion.290
  187.6 1.6 fusion.293
  189.9 1.6 fusion.294
  192.1 2.3 fusion.295
  204.0 1.6 fusion.289
  206.3 1.6 fusion.290
  208.6 1.6 fusion.291
  210.8 1.6 fusion.292
  215.4 1.6 fusion.294
  217.7 2.3 fusion.295
  229.5 1.6 fusion.289
  231.9 1.6 fusion.290
  238.6 1.6 fusion.293
  241.0 1.6 fusion.294
  243.2 2.3 fusion.295
  252.8 1.6 fusion.288
  259.7 1.6 fusion.291
  261.9 1.6 fusion.292
  266.5 1.6 fusion.294
  268.8 2.3 fusion.295
  280.6 1.6 fusion.289
  283.0 1.6 fusion.290
  289.7 1.6 fusion.293
  292.1 1.6 fusion.294
  294.3 2.3 fusion.295
  296.6 3.0 reshape.126
  299.5 2.5 fusion.208
  302.4 3.7 %convolution_bitcast_fusion.2 = f32[4,64,32]{1,2,0:T(8,128)} fusion(f32[4,8,64,32]{3,2,1,0:T(8,128)S(1)} %reshape.115, f32[4,8,64,64]{3,2,1,0:T(8,128)} %param.16), kind=kOutput, calls=%fused_computation.187 | convolution fusion | flops 50331648 | bytes 819200 | tf_op jit(solution)/shard_map/qkab,qkbc->qac/dot_general | solution.py:67
  306.0 3.9 %fusion.206 = f32[64,2048]{1,0:T(8,128)S(1)} fusion(f32[512,2048]{1,0:T(8,128)} %all-gather.4.cloned.1.call-done, s32[64]{0:T(128)S(1)} %eq.30), kind=kOutput, calls=%fused_computation.196 | convolution fusion | flops 805339136 | bytes 4718848 | tf_op jit(solution)/shard_map/dot_general | solution.py:29
  310.0 2.0 reshape.112
  312.0 5.1 %convolution_bitcast_fusion.1 = f32[8,32,64]{2,1,0:T(8,128)S(1)} fusion(f32[8,8,64,32]{3,2,1,0:T(8,128)} %reshape.112, f32[8,8,64,64]{3,2,1,0:T(8,128)S(1)} %copy-done), kind=kOutput, calls=%fused_computation.186 | convolution fusion | flops 100663296 | bytes 1638400 | tf_op jit(solution)/shard_map/lkab,lkbc->lac/dot_general | solution.py:54
  (117 shorter events, 53.1 us)
Async XLA Ops:
  6.5 305.5 %copy-start = (f32[8,8,64,64]{3,2,1,0:T(8,128)S(1)}, f32[8,8,64,64]{3,2,1,0:T(8,128)}, u32[]{:S(2)}) copy-start(f32[8,8,64,64]{3,2,1,0:T(8,128)} %param.14) | copy-start | bytes 3145732
  6.5 290.0 %all-gather.6.cloned.1.call-start = ((), (), s32[]{:S(2)}) async-start(), calls=%async_computation.1 | async-start | bytes 2129920 | tf_op jit(solution)/shard_map/all_gather | solution.py:63
  10.3 295.8 %all-gather.4.cloned.1.call-start = ((), (), s32[]{:S(2)}) async-start(), calls=%async_computation | async-start | bytes 4259840 | tf_op jit(solution)/shard_map/all_gather | solution.py:52
  10.3 52.2 %collective-permute-start = (bf16[2048,784]{0,1:T(8,128)(2,1)}, bf16[2048,784]{0,1:T(8,128)(2,1)}, u32[]{:S(2)}, u32[]{:S(2)}) collective-permute-start(bf16[2048,784]{0,1:T(8,128)(2,1)} %param.11), channel_id=1, source_target_pairs={{0,4},{4,8},{8,12},{12,16},{16,20},{20,24},{24,28},{28,32},{32,36}... | collective-permute-start | bytes 9633800 | tf_op jit(solution)/shard_map/ppermute | solution.py:17
  15.6 53.0 %collective-permute-start.1 = (bf16[2048,784]{0,1:T(8,128)(2,1)}, bf16[2048,784]{0,1:T(8,128)(2,1)}, u32[]{:S(2)}, u32[]{:S(2)}) collective-permute-start(bf16[2048,784]{0,1:T(8,128)(2,1)} %param.11), channel_id=1, source_target_pairs={{4,0},{8,4},{12,8},{16,12},{20,16},{24,20},{28,24},{32,28},{36,32}... | collective-permute-start | bytes 9633800 | tf_op jit(solution)/shard_map/ppermute | solution.py:20
  17.5 35.9 %collective-permute-start.2 = (bf16[2048,32]{0,1:T(8,128)(2,1)}, bf16[2048,32]{0,1:T(8,128)(2,1)S(1)}, u32[]{:S(2)}, u32[]{:S(2)}) collective-permute-start(bf16[2048,32]{0,1:T(8,128)(2,1)} %param.12), channel_id=1, source_target_pairs={{0,4},{4,8},{8,12},{12,16},{16,20},{20,24},{24,28},{28,32},{32,36}... | collective-permute-start | bytes 393224 | tf_op jit(solution)/shard_map/ppermute | solution.py:17
  24.5 36.6 %collective-permute-start.3 = (bf16[2048,32]{0,1:T(8,128)(2,1)}, bf16[2048,32]{0,1:T(8,128)(2,1)S(1)}, u32[]{:S(2)}, u32[]{:S(2)}) collective-permute-start(bf16[2048,32]{0,1:T(8,128)(2,1)} %param.12), channel_id=1, source_target_pairs={{4,0},{8,4},{12,8},{16,12},{20,16},{24,20},{28,24},{32,28},{36,32}... | collective-permute-start | bytes 393224 | tf_op jit(solution)/shard_map/ppermute | solution.py:20
  27.3 8.6 %copy-start.9 = (s32[4,8]{1,0:T(4,128)S(1)}, s32[4,8]{1,0:T(4,128)}, u32[]{:S(2)}) copy-start(s32[4,8]{1,0:T(4,128)} %param.18) | copy-start | bytes 388
  27.3 8.7 %copy-start.8 = (s32[8,8]{1,0:T(8,128)S(1)}, s32[8,8]{1,0:T(8,128)}, u32[]{:S(2)}) copy-start(s32[8,8]{1,0:T(8,128)} %param.17) | copy-start | bytes 772
  27.3 8.8 %copy-start.7 = (s32[8,8]{1,0:T(8,128)S(1)}, s32[8,8]{1,0:T(8,128)}, u32[]{:S(2)}) copy-start(s32[8,8]{1,0:T(8,128)} %param.19) | copy-start | bytes 772
  27.4 33.7 %copy-start.3 = (bf16[2048,32]{0,1:T(8,128)(2,1)S(1)}, bf16[2048,32]{0,1:T(8,128)(2,1)}, u32[]{:S(2)}) copy-start(bf16[2048,32]{0,1:T(8,128)(2,1)} %param.12) | copy-start | bytes 393220
  62.6 4.2 %copy-start.1 = (bf16[2048,784]{0,1:T(8,128)(2,1)S(1)}, bf16[2048,784]{0,1:T(8,128)(2,1)}, u32[]{:S(2)}) copy-start(bf16[2048,784]{0,1:T(8,128)(2,1)} %param.11) | copy-start | bytes 9633796
  310.0 7.2 %copy-start.4 = (f32[8,64,64]{2,1,0:T(8,128)S(1)}, f32[8,64,64]{2,1,0:T(8,128)}, u32[]{:S(2)}) copy-start(f32[8,64,64]{2,1,0:T(8,128)} %param.15) | copy-start | bytes 393220
  310.0 7.7 %copy-start.2 = (f32[8,256,64]{1,2,0:T(8,128)S(1)}, f32[8,256,64]{1,2,0:T(8,128)}, u32[]{:S(2)}) copy-start(f32[8,256,64]{1,2,0:T(8,128)} %param.13) | copy-start | bytes 1572868
  312.0 5.1 %copy-start.6 = (f32[4,64,32]{1,2,0:T(8,128)S(1)}, f32[4,64,32]{1,2,0:T(8,128)}, u32[]{:S(2)}) copy-start(f32[4,64,32]{1,2,0:T(8,128)} %convolution_bitcast_fusion.2) | copy-start | bytes 98308
  312.0 6.1 %copy-start.5 = (f32[8,256,32]{1,2,0:T(8,128)S(1)}, f32[8,256,32]{1,2,0:T(8,128)}, u32[]{:S(2)}) copy-start(f32[8,256,32]{1,2,0:T(8,128)} %get-tuple-element.52) | copy-start | bytes 786436
Sparse Core Ops, SparseCore 0:
  10.4 77.7 all-gather.5
  90.9 76.2 all-gather.3
where the time goes:
time: 329 us; the launch traced here: 326 us
  matrix products  129 us (39%)
  loops' own time  82.8 us (25%)
  local copies, waits for them, and re-layouts  50.3 us (15%)
  waiting for transfers between devices  24.9 us (8%)
  starting transfers between devices  16.1 us (5%)
  between operations  13.6 us (4%)
  other arithmetic  9.25 us (3%)
    dot_general x64, matrix products, near_tiles(): jnp.dot(kernel, near_vectors, preferred_element_type=jnp.float32)  110 us
    another operation x1, loops' own time, local(): lax.map(partial(near_tiles, window_vectors), (point_blocks, norm_blocks,...  82.8 us
    ppermute x2, waiting for transfers between devices, with_halo(): lax.ppermute(lax.slice_in_dim(block, block.shape[dim] - width, None, axis...  17.3 us
    unnamed x25, local copies, waits for them, and re-layouts  15.7 us
    while x2, local copies, waits for them, and re-layouts, local(): lax.map(partial(near_tiles, window_vectors), (point_blocks, norm_blocks,...  15 us
    ppermute x2, starting transfers between devices, with_halo(): lax.ppermute(lax.slice_in_dim(block, block.shape[dim] - width, None, axis...  12.2 us
    ppermute x2, waiting for transfers between devices, with_halo(): lax.ppermute(lax.slice_in_dim(block, 0, width, axis=dim), axis, backward)  7.62 us
  transfers between devices with their start and end apart: 6, of which 2 were waited for; matrix products, arithmetic and copies ran while one was open for 53% of the time, Pallas kernels for 0%

commit v1 on v0

v1 whole, which is shorter than its diff:
```python
import functools
import math

import jax
import jax.numpy as jnp
from jax import lax
from jax.experimental import pallas as pl
from jax.experimental.pallas import tpu as pltpu
from jax.sharding import PartitionSpec as P

MESH = pl.DeviceIdType.MESH
F32 = jnp.float32
BF16 = jnp.bfloat16
RIDGE = 0.5
NN = (((1,), (0,)), ((), ()))
NT = (((1,), (1,)), ((), ()))


def mm(a, b, dims=NN):
    return lax.dot_general(a, b, dims, preferred_element_type=F32)


def split(w):
    high = w.astype(BF16)
    return high, (w - high.astype(F32)).astype(BF16)


def kernel(
    dims,
    pts, vt, bases, lc, tr, uc, fl, fu, nl,
    out,
    pv, hp, vall, hv, nlr, masks, bv, lv, tv, uv, gat, wl, wu, halves,
    ncol, nrow, acc, hacc, hsend, hres, asend, arecv,
    lsem, hp_s, hp_r, v_s, v_r, nl_s, nl_r, hv_s, hv_r, z_s, z_r, x_s, x_r, c_s, c_r, hs_s, hs_r, a_s, a_r,
):
    zdim, xdim, ydim = dims
    n = zdim * xdim * 2
    d = lax.axis_index("leaf")
    r = lax.axis_index("rhs")
    core = lax.rem(d, 2)
    x = lax.rem(lax.div(d, 2), xdim)
    z = lax.div(d, 2 * xdim)
    nxt = lax.rem(d + 1, n)
    prv = lax.rem(d + n - 1, n)

    def leaf_at(zz, xx, cc):
        return (zz * xdim + xx) * 2 + cc

    def rc(src, dst, ssem, rsem, leaf, rhs):
        return pltpu.make_async_remote_copy(
            src_ref=src, dst_ref=dst, send_sem=ssem, recv_sem=rsem,
            device_id=(leaf, rhs), device_id_type=MESH,
        )

    leaves = pts.shape[0]
    leaf_pts = pts.shape[1]
    features = pts.shape[2]
    cols = vt.shape[1]
    rank = bases.shape[2]
    scale = math.log2(math.e) / features

    barrier = pltpu.get_barrier_semaphore()
    partners = [(nxt, r), (prv, r)]
    partners += [(d, lax.rem(r + j, ydim)) for j in range(1, ydim)]
    partners += [(leaf_at(lax.rem(z + s, zdim), x, core), r) for s in range(1, zdim)]
    partners += [(leaf_at(z, lax.rem(x + j, xdim), core), r) for j in range(1, xdim)]
    partners += [(leaf_at(z, x, 1 - core), r)]
    for who in partners:
        pl.semaphore_signal(barrier, inc=1, device_id=who, device_id_type=MESH)

    loads = [
        pltpu.make_async_copy(vt, vall.at[r], lsem.at[0]),
        pltpu.make_async_copy(bases, bv, lsem.at[1]),
        pltpu.make_async_copy(tr, tv, lsem.at[2]),
        pltpu.make_async_copy(pts, pv, lsem.at[3]),
        pltpu.make_async_copy(lc, lv, lsem.at[4]),
        pltpu.make_async_copy(uc, uv, lsem.at[5]),
    ]
    for copy in loads:
        copy.start()

    pl.semaphore_wait(barrier, len(partners))

    half_leaves = leaves // 2
    points_out = [
        rc(pts.at[r], hp.at[0], hp_s.at[0], hp_r.at[0], prv, r),
        rc(pts.at[half_leaves + r], hp.at[1], hp_s.at[1], hp_r.at[1], nxt, r),
    ]
    lists_out = [
        rc(nl, nlr.at[0], nl_s.at[0], nl_r.at[0], prv, r),
        rc(nl, nlr.at[1], nl_s.at[1], nl_r.at[1], nxt, r),
    ]
    vectors_out = [
        rc(vt, vall.at[r], v_s.at[j - 1], v_r.at[j - 1], d, lax.rem(r + j, ydim)) for j in range(1, ydim)
    ]
    for copy in vectors_out + points_out + lists_out:
        copy.start()

    loads[0].wait()
    loads[1].wait()
    loads[2].wait()
    coeffs = []
    for i in range(leaves):
        bh, bl = split(bv[i])
        v = vall[r, i]
        coeffs.append(mm(v, bh) + mm(v, bl))
    parents = []
    for i in range(leaves):
        th, tl = split(tv[i])
        ch, cl = split(coeffs[i])
        lifted = mm(ch, th) + (mm(cl, th) + mm(ch, tl))
        if i % 2 == 0:
            parents.append(lifted)
        else:
            parents[-1] = parents[-1] + lifted
    parts = coeffs + parents
    for m in range(len(parts) // 2):
        gat[z, x, core, m] = jnp.concatenate(parts[2 * m : 2 * m + 2], axis=1).astype(BF16)

    nl_own = nl[...]
    lane = lax.broadcasted_iota(jnp.int32, (leaves, 128), 1) + (d - 1) * leaves

    def mask_of(lists):
        total = jnp.zeros((leaves, 128), F32)
        for k in range(lists.shape[1]):
            entry = lists[:, k : k + 1]
            total = total + jnp.where((entry == lane) & (entry >= 0), 1.0, 0.0).astype(F32)
        return total

    masks[2] = mask_of(nl_own)
    lane_half = lax.broadcasted_iota(jnp.int32, (cols, 128), 1)
    halves[0] = jnp.where(lane_half < rank, 1.0, 0.0).astype(BF16)
    halves[1] = jnp.where(lane_half < rank, 0.0, 1.0).astype(BF16)

    loads[3].wait()

    def norms(index, block):
        wide = block.astype(F32)
        col = jnp.broadcast_to(jnp.sum(wide * wide, axis=1, keepdims=True) * (-scale), (leaf_pts, 128))
        ncol[index] = col
        nrow[index] = jnp.transpose(col)[0:1, :]

    for i in range(leaves):
        norms(i, pv[i])

    order = sorted(range(1, zdim), key=lambda s: (min(s, zdim - s), s))
    z_out = {
        s: rc(
            gat.at[z, x, core], gat.at[z, x, core], z_s.at[s], z_r.at[s],
            leaf_at(lax.rem(z + s, zdim), x, core), r,
        )
        for s in order
    }
    for s in order:
        z_out[s].start()

    x_out = []

    def forward(s):
        zz = lax.rem(z + zdim - s, zdim)
        block = gat.at[zz, x, core]
        if s:
            rc(block, block, z_s.at[s], z_r.at[s], d, r).wait_recv()
        for j in range(1, xdim):
            copy = rc(
                block, block, x_s.at[s, j - 1], x_r.at[s, j - 1],
                leaf_at(z, lax.rem(x + j, xdim), core), r,
            )
            copy.start()
            x_out.append(copy)

    forward(0)
    for i in range(leaves):
        acc[i] = jnp.zeros((ydim, cols, leaf_pts), F32)
    hacc[...] = jnp.zeros((2, ydim * cols, leaf_pts), F32)

    for j in range(1, ydim):
        source = lax.rem(r + ydim - j, ydim)
        rc(vt, vall.at[source], v_s.at[j - 1], v_r.at[j - 1], d, r).wait_recv()
    hv_out = [
        rc(vall.at[:, r], hv.at[0], hv_s.at[0], hv_r.at[0], prv, r),
        rc(vall.at[:, half_leaves + r], hv.at[1], hv_s.at[1], hv_r.at[1], nxt, r),
    ]
    for copy in hv_out:
        copy.start()

    lane1 = lax.broadcasted_iota(jnp.int32, (1, 128), 1)

    def mask_at(which, row, w):
        values = masks[which, pl.ds(row, 1), :]
        return jnp.sum(jnp.where(lane1 == w, values, 0.0), axis=1, keepdims=True).astype(BF16)

    def tile_of(xa, xb, ia, ib):
        cross = mm(xa, xb, NT)
        col = ncol[ia]
        return jnp.exp2(cross * (2.0 * scale) + (jnp.concatenate([col, col], axis=1) + nrow[ib])).astype(BF16)

    wide = (ydim * cols, leaf_pts)

    def add(i, value):
        acc[i] = acc[i] + value.reshape(ydim, cols, leaf_pts)

    def own_pair(t):
        shift = t // 2
        a = 2 * r + t % 2 if t < leaves else r
        b = lax.rem(a + shift, leaves)
        tile = tile_of(pv[a], pv[b], a, b)
        vb = vall[:, b].reshape(wide)
        add(a, mm(vb * mask_at(2, a, leaves + b), tile, NT))
        if shift:
            va = vall[:, a].reshape(wide)
            add(b, mm(va * mask_at(2, b, leaves + a), tile, NN))

    for t in range(leaves + 1):
        own_pair(t)
        if t < zdim - 1:
            forward(order[t])

    c_out = []

    def to_sibling(j):
        column = gat.at[:, lax.rem(x + xdim - j, xdim), core]
        copy = rc(column, column, c_s.at[j], c_r.at[j], leaf_at(z, x, 1 - core), r)
        copy.start()
        c_out.append(copy)

    to_sibling(0)

    for h in range(2):
        points_out[h].wait_recv()
        lists_out[h].wait_recv()
        rc(vall.at[:, r], hv.at[h], hv_s.at[h], hv_r.at[h], d, r).wait_recv()
        masks[h] = mask_of(nlr[h])
        norms(leaves + h, hp[h])

    def halo_pair(p, carry):
        side = lax.div(p + r, leaves)
        o = p + r - half_leaves * side
        tile = tile_of(pv[o], hp[side], o, leaves + side)
        vh = hv[side].reshape(wide)
        add(o, mm(vh * mask_at(2, o, 2 * leaves + r - (leaves + half_leaves) * side), tile, NT))
        vo = vall[:, o].reshape(wide)
        hacc[side] = hacc[side] + mm(vo * mask_at(side, r + half_leaves * side, leaves + o), tile, NN)
        return carry

    for p in range(leaves + 1):
        halo_pair(p, 0)
    hsend[...] = hacc[...].reshape(2, ydim, cols, leaf_pts).astype(BF16)

    loads[4].wait()
    loads[5].wait()

    def widen(dst, src, i):
        for k in range(8):
            w = src[i * 8 + k]
            dst[i, :, 2 * rank * k : 2 * rank * (k + 1)] = jnp.concatenate([w, w], axis=1).astype(BF16)

    widen(wu, uv, 0)
    hs_out = [
        rc(hsend.at[0], hres.at[0], hs_s.at[0], hs_r.at[0], nxt, r),
        rc(hsend.at[1], hres.at[1], hs_s.at[1], hs_r.at[1], prv, r),
    ]
    for copy in hs_out:
        copy.start()
    for q in range(1, leaves // 2):
        widen(wu, uv, q)

    for h in range(2):
        hs_out[h].wait_recv()
        i = r + half_leaves * h
        acc[i] = acc[i] + hres[h].astype(F32)
    for j in range(1, ydim):
        target = lax.rem(r + j, ydim)
        for i in range(leaves):
            asend[j - 1, i] = acc[i, target].astype(BF16)
    widen(wl, lv, 0)
    a_out = [
        rc(asend.at[j - 1], arecv.at[j - 1], a_s.at[j - 1], a_r.at[j - 1], d, lax.rem(r + j, ydim))
        for j in range(1, ydim)
    ]
    for copy in a_out:
        copy.start()
    for i in range(1, leaves):
        widen(wl, lv, i)

    for j in range(1, xdim):
        for s in range(zdim):
            block = gat.at[lax.rem(z + zdim - s, zdim), lax.rem(x + xdim - j, xdim), core]
            rc(block, block, x_s.at[s, j - 1], x_r.at[s, j - 1], d, r).wait_recv()
        to_sibling(j)
    for j in range(ydim - 1):
        a_out[j].wait_recv()
    for j in range(xdim):
        column = gat.at[:, lax.rem(x + xdim - j, xdim), 1 - core]
        rc(column, column, c_s.at[j], c_r.at[j], d, r).wait_recv()

    def gathered(index, per_device, first):
        device = lax.div(index, per_device)
        inner = lax.rem(index, per_device)
        block = gat[
            lax.div(device, 2 * xdim), lax.rem(lax.div(device, 2), xdim), lax.rem(device, 2), first + lax.div(inner, 2)
        ]
        return block * halves[lax.rem(inner, 2)]

    for q in range(leaves // 2):
        left = jnp.concatenate([gathered(fu[q, k], leaves // 2, leaves // 2) for k in range(8)], axis=1)
        upper = mm(left, wu[q], NT)
        uh, ul = split(upper)
        for i in (2 * q, 2 * q + 1):
            left = jnp.concatenate([gathered(fl[i, k], leaves, 0) for k in range(8)], axis=1)
            th, tl = split(tv[i])
            field = mm(left, wl[i], NT) + (mm(uh, th, NT) + mm(ul, th, NT) + mm(uh, tl, NT))
            fh, fo = split(field)
            bh, bl = split(bv[i])
            far = mm(fh, bh, NT) + (mm(fo, bh, NT) + mm(fh, bl, NT))
            near = acc[i, r]
            for j in range(ydim - 1):
                near = near + arecv[j, i].astype(F32)
            out[i] = near + far + RIDGE * vall[r, i].astype(F32)

    for copy in vectors_out + points_out + lists_out + hv_out + hs_out + a_out + x_out + c_out:
        copy.wait_send()
    for s in order:
        z_out[s].wait_send()


def solution(mesh):
    n = mesh.shape["leaf"]
    ydim = mesh.shape["rhs"]
    xdim = 4 if n >= 32 else 2
    zdim = n // (2 * xdim)

    def local(points, vectors, bases, leaf_coupling, transfer, up_coupling, far_leaf, far_up, near_lists):
        leaves, leaf_pts, rank = bases.shape
        cols = vectors.shape[1]
        features = points.shape[1]
        vt = jnp.transpose(vectors.reshape(leaves, leaf_pts, cols), (0, 2, 1))
        anywhere = pl.BlockSpec(memory_space=pl.ANY)
        vmem = pl.BlockSpec(memory_space=pltpu.VMEM)
        smem = pl.BlockSpec(memory_space=pltpu.SMEM)
        dma = pltpu.SemaphoreType.DMA
        wide = ydim * cols
        outT = pl.pallas_call(
            functools.partial(kernel, (zdim, xdim, ydim)),
            out_shape=jax.ShapeDtypeStruct((leaves, cols, leaf_pts), F32),
            in_specs=[anywhere] * 6 + [smem, smem, vmem],
            out_specs=vmem,
            scratch_shapes=[
                pltpu.VMEM((leaves, leaf_pts, features), BF16),
                pltpu.VMEM((2, leaf_pts, features), BF16),
                pltpu.VMEM((ydim, leaves, cols, leaf_pts), BF16),
                pltpu.VMEM((2, ydim, cols, leaf_pts), BF16),
                pltpu.VMEM((2,) + near_lists.shape, jnp.int32),
                pltpu.VMEM((3, leaves, 128), F32),
                pltpu.VMEM(bases.shape, F32),
                pltpu.VMEM((leaves * 8, rank, rank), F32),
                pltpu.VMEM(transfer.shape, F32),
                pltpu.VMEM((leaves * 4, rank, rank), F32),
                pltpu.VMEM((zdim, xdim, 2, leaves * 3 // 4, cols, 2 * rank), BF16),
                pltpu.VMEM((leaves, rank, 16 * rank), BF16),
                pltpu.VMEM((leaves // 2, rank, 16 * rank), BF16),
                pltpu.VMEM((2, cols, 2 * rank), BF16),
                pltpu.VMEM((leaves + 2, leaf_pts, 128), F32),
                pltpu.VMEM((leaves + 2, 1, leaf_pts), F32),
                pltpu.VMEM((leaves, ydim, cols, leaf_pts), F32),
                pltpu.VMEM((2, wide, leaf_pts), F32),
                pltpu.VMEM((2, ydim, cols, leaf_pts), BF16),
                pltpu.VMEM((2, ydim, cols, leaf_pts), BF16),
                pltpu.VMEM((ydim - 1, leaves, cols, leaf_pts), BF16),
                pltpu.VMEM((ydim - 1, leaves, cols, leaf_pts), BF16),
                dma((6,)),
                dma((2,)), dma((2,)),
                dma((ydim - 1,)), dma((ydim - 1,)),
                dma((2,)), dma((2,)),
                dma((2,)), dma((2,)),
                dma((zdim,)), dma((zdim,)),
                dma((zdim, xdim - 1)), dma((zdim, xdim - 1)),
                dma((xdim,)), dma((xdim,)),
                dma((2,)), dma((2,)),
                dma((ydim - 1,)), dma((ydim - 1,)),
            ],
            compiler_params=pltpu.CompilerParams(
                collective_id=0, has_side_effects=True, vmem_limit_bytes=56 * 1024 * 1024
            ),
        )(
            points.reshape(leaves, leaf_pts, features),
            vt,
            bases,
            leaf_coupling.reshape(-1, rank, rank),
            transfer,
            up_coupling.reshape(-1, rank, rank),
            far_leaf,
            far_up,
            near_lists,
        )
        return jnp.transpose(outT, (0, 2, 1)).reshape(leaves * leaf_pts, cols)

    return jax.shard_map(
        local,
        mesh=mesh,
        in_specs=(
            P("leaf", None),
            P("leaf", "rhs"),
            P("leaf", None, None),
            P("leaf", None, None, None),
            P("leaf", None, None),
            P("leaf", None, None, None),
            P("leaf", None),
            P("leaf", None),
            P("leaf", None),
        ),
        out_specs=P("leaf", "rhs"),
        check_vma=False,
    )
```

time: 329 us -> 60.6 us (0.18)
  the two profiles are of different devices: /device:TPU:127 before, /device:TPU:1 now
where the time goes in v1:
time: 60.6 us; the launch traced here: 60.3 us
  Pallas kernels  48.7 us (80%)
  local copies, waits for them, and re-layouts  11.6 us (19%)
    pallas_call x1, Pallas kernels, local(): pl.pallas_call(functools.partial(kernel, (zdim, xdim, ydim)), out_shape=j...  48.7 us
    unnamed x2, local copies, waits for them, and re-layouts  8.32 us
    reshape x1, local copies, waits for them, and re-layouts, local(): return jnp.transpose(outT, (0, 2, 1)).reshape(leaves * leaf_pts, cols)  1.67 us
    reshape x1, local copies, waits for them, and re-layouts, local(): vt = jnp.transpose(vectors.reshape(leaves, leaf_pts, cols), (0, 2, 1))  1.57 us

profile of v1, /device:TPU:1, one launch (start us, length us, event | category | flops | bytes accessed | tf_op | source)
XLA Modules:
  0.0 60.3 jit_solution(5206584845457918721)
XLA Ops:
  0.0 1.6 %copy.19 = bf16[4,8,8,256]{3,2,0,1:T(8,128)(2,1)} copy(bf16[4,8,8,256]{3,2,1,0:T(8,128)(2,1)} %bitcast.18) | data formatting | bytes 262144 | tf_op jit(solution)/shard_map/reshape | solution.py:337
  1.6 2.3 %copy.14.bases = f32[8,256,64]{2,1,0:T(8,128)} copy(f32[8,256,64]{1,2,0:T(8,128)} %param.11) | data formatting | bytes 1048576 | tf_op args[2]
  3.9 6.0 %copy.12 = bf16[2048,784]{1,0:T(8,128)(2,1)} copy(bf16[2048,784]{0,1:T(8,128)(2,1)} %param.9) | data formatting | bytes 6422528 | tf_op args[0]
  9.9 48.7 %shard_map.91 = f32[8,32,256]{2,1,0:T(8,128)} custom-call(bf16[8,256,784]{2,1,0:T(8,128)(2,1)} %bitcast.13, bf16[8,32,256]{2,1,0:T(8,128)(2,1)} %bitcast.17, f32[8,256,64]{2,1,0:T(8,128)} %copy.14.bases, f32[64,64,64]{2,1,0:T(8,128)} %bitcast.14, f32[8,64,64]{2,1,0:T(8,128)} %tr.1, f32[32,64,64]{2,1,0:T(8,128)} %bitcast.16, s32[8,8]{1,0:T(8,128)} %fl.1, ...), custom_call_target="tpu_custom_call" | custom-call | tf_op jit(solution)/shard_map/pallas_call | solution.py:343
  58.6 1.7 %copy.17 = f32[8,4,8,256]{3,2,0,1:T(8,128)} copy(f32[8,4,8,256]{3,2,1,0:T(8,128)} %bitcast.15) | data formatting | bytes 524288 | tf_op jit(solution)/shard_map/reshape | solution.py:396

commit v2 on v1

--- a/solution.py
+++ b/solution.py
@@ -29,7 +29,7 @@
     dims,
     pts, vt, bases, lc, tr, uc, fl, fu, nl,
     out,
-    pv, hp, vall, hv, nlr, masks, bv, lv, tv, uv, gat, wl, wu, halves,
+    pt, pv, hp, vall, hv, nlr, masks, bv, lv, tv, uv, gat, wl, wu, halves,
     ncol, nrow, acc, hacc, hsend, hres, asend, arecv,
     lsem, hp_s, hp_r, v_s, v_r, nl_s, nl_r, hv_s, hv_r, z_s, z_r, x_s, x_r, c_s, c_r, hs_s, hs_r, a_s, a_r,
 ):
@@ -52,18 +52,18 @@
             device_id=(leaf, rhs), device_id_type=MESH,
         )
 
-    leaves = pts.shape[0]
-    leaf_pts = pts.shape[1]
-    features = pts.shape[2]
-    cols = vt.shape[1]
-    rank = bases.shape[2]
+    leaves, rank, leaf_pts = bases.shape
+    features = pts.shape[0]
+    cols = vt.shape[0]
     scale = math.log2(math.e) / features
 
     barrier = pltpu.get_barrier_semaphore()
     partners = [(nxt, r), (prv, r)]
     partners += [(d, lax.rem(r + j, ydim)) for j in range(1, ydim)]
     partners += [(leaf_at(lax.rem(z + s, zdim), x, core), r) for s in range(1, zdim)]
-    partners += [(leaf_at(z, lax.rem(x + j, xdim), core), r) for j in range(1, xdim)]
+    right, left = lax.rem(x + 1, xdim), lax.rem(x + xdim - 1, xdim)
+    across = lax.rem(x + 2, xdim)
+    partners += [(leaf_at(z, right, core), r), (leaf_at(z, left, core), r)]
     partners += [(leaf_at(z, x, 1 - core), r)]
     for who in partners:
         pl.semaphore_signal(barrier, inc=1, device_id=who, device_id_type=MESH)
@@ -72,7 +72,7 @@
         pltpu.make_async_copy(vt, vall.at[r], lsem.at[0]),
         pltpu.make_async_copy(bases, bv, lsem.at[1]),
         pltpu.make_async_copy(tr, tv, lsem.at[2]),
-        pltpu.make_async_copy(pts, pv, lsem.at[3]),
+        pltpu.make_async_copy(pts, pt, lsem.at[3]),
         pltpu.make_async_copy(lc, lv, lsem.at[4]),
         pltpu.make_async_copy(uc, uv, lsem.at[5]),
     ]
@@ -81,10 +81,13 @@
 
     pl.semaphore_wait(barrier, len(partners))
 
+    def block_of(i):
+        return pl.ds(pl.multiple_of(i * leaf_pts, leaf_pts), leaf_pts)
+
     half_leaves = leaves // 2
     points_out = [
-        rc(pts.at[r], hp.at[0], hp_s.at[0], hp_r.at[0], prv, r),
-        rc(pts.at[half_leaves + r], hp.at[1], hp_s.at[1], hp_r.at[1], nxt, r),
+        rc(pts.at[:, block_of(r)], hp.at[0], hp_s.at[0], hp_r.at[0], prv, r),
+        rc(pts.at[:, block_of(half_leaves + r)], hp.at[1], hp_s.at[1], hp_r.at[1], nxt, r),
     ]
     lists_out = [
         rc(nl, nlr.at[0], nl_s.at[0], nl_r.at[0], prv, r),
@@ -102,8 +105,8 @@
     coeffs = []
     for i in range(leaves):
         bh, bl = split(bv[i])
-        v = vall[r, i]
-        coeffs.append(mm(v, bh) + mm(v, bl))
+        v = vall[r, :, block_of(i)]
+        coeffs.append(mm(v, bh, NT) + mm(v, bl, NT))
     parents = []
     for i in range(leaves):
         th, tl = split(tv[i])
@@ -136,12 +139,13 @@
 
     def norms(index, block):
         wide = block.astype(F32)
-        col = jnp.broadcast_to(jnp.sum(wide * wide, axis=1, keepdims=True) * (-scale), (leaf_pts, 128))
-        ncol[index] = col
-        nrow[index] = jnp.transpose(col)[0:1, :]
+        row = jnp.sum(wide * wide, axis=0, keepdims=True) * (-scale)
+        nrow[index] = row
+        if index < leaves:
+            ncol[index] = jnp.transpose(jnp.broadcast_to(row, (128, leaf_pts)))
 
     for i in range(leaves):
-        norms(i, pv[i])
+        norms(i, pt[:, block_of(i)])
 
     order = sorted(range(1, zdim), key=lambda s: (min(s, zdim - s), s))
     z_out = {
@@ -155,19 +159,33 @@
         z_out[s].start()
 
     x_out = []
+    steps = [0] + order
+
+    def x_send(s, column, kind, target):
+        block = gat.at[lax.rem(z + zdim - s, zdim), column, core]
+        copy = rc(block, block, x_s.at[s, kind], x_r.at[s, kind], leaf_at(z, target, core), r)
+        copy.start()
+        x_out.append(copy)
+
+    def x_wait(s, column, kind):
+        block = gat.at[lax.rem(z + zdim - s, zdim), column, core]
+        rc(block, block, x_s.at[s, kind], x_r.at[s, kind], d, r).wait_recv()
 
     def forward(s):
-        zz = lax.rem(z + zdim - s, zdim)
-        block = gat.at[zz, x, core]
         if s:
+            block = gat.at[lax.rem(z + zdim - s, zdim), x, core]
             rc(block, block, z_s.at[s], z_r.at[s], d, r).wait_recv()
-        for j in range(1, xdim):
-            copy = rc(
-                block, block, x_s.at[s, j - 1], x_r.at[s, j - 1],
-                leaf_at(z, lax.rem(x + j, xdim), core), r,
-            )
-            copy.start()
-            x_out.append(copy)
+        x_send(s, x, 0, right)
+        x_send(s, x, 1, left)
+
+    def relay(m):
+        s = steps[m]
+        if m % 2 == 0:
+            x_wait(s, left, 0)
+            x_send(s, left, 2, right)
+        else:
+            x_wait(s, right, 1)
+            x_send(s, right, 2, left)
 
     forward(0)
     for i in range(leaves):
@@ -178,8 +196,8 @@
         source = lax.rem(r + ydim - j, ydim)
         rc(vt, vall.at[source], v_s.at[j - 1], v_r.at[j - 1], d, r).wait_recv()
     hv_out = [
-        rc(vall.at[:, r], hv.at[0], hv_s.at[0], hv_r.at[0], prv, r),
-        rc(vall.at[:, half_leaves + r], hv.at[1], hv_s.at[1], hv_r.at[1], nxt, r),
+        rc(vall.at[:, :, block_of(r)], hv.at[0], hv_s.at[0], hv_r.at[0], prv, r),
+        rc(vall.at[:, :, block_of(half_leaves + r)], hv.at[1], hv_s.at[1], hv_r.at[1], nxt, r),
     ]
     for copy in hv_out:
         copy.start()
@@ -191,7 +209,7 @@
         return jnp.sum(jnp.where(lane1 == w, values, 0.0), axis=1, keepdims=True).astype(BF16)
 
     def tile_of(xa, xb, ia, ib):
-        cross = mm(xa, xb, NT)
+        cross = mm(xa, xb)
         col = ncol[ia]
         return jnp.exp2(cross * (2.0 * scale) + (jnp.concatenate([col, col], axis=1) + nrow[ib])).astype(BF16)
 
@@ -204,32 +222,36 @@
         shift = t // 2
         a = 2 * r + t % 2 if t < leaves else r
         b = lax.rem(a + shift, leaves)
-        tile = tile_of(pv[a], pv[b], a, b)
-        vb = vall[:, b].reshape(wide)
+        tile = tile_of(pv[a], pt[:, block_of(b)], a, b)
+        vb = vall[:, :, block_of(b)].reshape(wide)
         add(a, mm(vb * mask_at(2, a, leaves + b), tile, NT))
         if shift:
-            va = vall[:, a].reshape(wide)
+            va = vall[:, :, block_of(a)].reshape(wide)
             add(b, mm(va * mask_at(2, b, leaves + a), tile, NN))
 
+    for i in range(leaves):
+        pv[i] = jnp.transpose(pt[:, block_of(i)])
     for t in range(leaves + 1):
         own_pair(t)
         if t < zdim - 1:
             forward(order[t])
+        if t >= 3:
+            relay(t - 3)
 
     c_out = []
 
-    def to_sibling(j):
-        column = gat.at[:, lax.rem(x + xdim - j, xdim), core]
-        copy = rc(column, column, c_s.at[j], c_r.at[j], leaf_at(z, x, 1 - core), r)
+    def to_sibling(m, j):
+        column = gat.at[:, j, core]
+        copy = rc(column, column, c_s.at[m], c_r.at[m], leaf_at(z, x, 1 - core), r)
         copy.start()
         c_out.append(copy)
 
-    to_sibling(0)
+    to_sibling(0, x)
 
     for h in range(2):
         points_out[h].wait_recv()
         lists_out[h].wait_recv()
-        rc(vall.at[:, r], hv.at[h], hv_s.at[h], hv_r.at[h], d, r).wait_recv()
+        rc(vall.at[:, :, block_of(r)], hv.at[h], hv_s.at[h], hv_r.at[h], d, r).wait_recv()
         masks[h] = mask_of(nlr[h])
         norms(leaves + h, hp[h])
 
@@ -239,12 +261,14 @@
         tile = tile_of(pv[o], hp[side], o, leaves + side)
         vh = hv[side].reshape(wide)
         add(o, mm(vh * mask_at(2, o, 2 * leaves + r - (leaves + half_leaves) * side), tile, NT))
-        vo = vall[:, o].reshape(wide)
+        vo = vall[:, :, block_of(o)].reshape(wide)
         hacc[side] = hacc[side] + mm(vo * mask_at(side, r + half_leaves * side, leaves + o), tile, NN)
         return carry
 
     for p in range(leaves + 1):
         halo_pair(p, 0)
+        if p < 2:
+            relay(6 + p)
     hsend[...] = hacc[...].reshape(2, ydim, cols, leaf_pts).astype(BF16)
 
     loads[4].wait()
@@ -283,16 +307,20 @@
     for i in range(1, leaves):
         widen(wl, lv, i)
 
-    for j in range(1, xdim):
-        for s in range(zdim):
-            block = gat.at[lax.rem(z + zdim - s, zdim), lax.rem(x + xdim - j, xdim), core]
-            rc(block, block, x_s.at[s, j - 1], x_r.at[s, j - 1], d, r).wait_recv()
-        to_sibling(j)
+    for m in range(1, zdim, 2):
+        x_wait(steps[m], left, 0)
+    to_sibling(1, left)
+    for m in range(0, zdim, 2):
+        x_wait(steps[m], right, 1)
+    to_sibling(2, right)
+    for m in range(zdim):
+        x_wait(steps[m], across, 2)
+    to_sibling(3, across)
     for j in range(ydim - 1):
         a_out[j].wait_recv()
-    for j in range(xdim):
-        column = gat.at[:, lax.rem(x + xdim - j, xdim), 1 - core]
-        rc(column, column, c_s.at[j], c_r.at[j], d, r).wait_recv()
+    for m, j in enumerate((x, left, right, across)):
+        column = gat.at[:, j, 1 - core]
+        rc(column, column, c_s.at[m], c_r.at[m], d, r).wait_recv()
 
     def gathered(index, per_device, first):
         device = lax.div(index, per_device)
@@ -312,11 +340,11 @@
             field = mm(left, wl[i], NT) + (mm(uh, th, NT) + mm(ul, th, NT) + mm(uh, tl, NT))
             fh, fo = split(field)
             bh, bl = split(bv[i])
-            far = mm(fh, bh, NT) + (mm(fo, bh, NT) + mm(fh, bl, NT))
+            far = mm(fh, bh) + (mm(fo, bh) + mm(fh, bl))
             near = acc[i, r]
             for j in range(ydim - 1):
                 near = near + arecv[j, i].astype(F32)
-            out[i] = near + far + RIDGE * vall[r, i].astype(F32)
+            out[:, block_of(i)] = near + far + RIDGE * vall[r, :, block_of(i)].astype(F32)
 
     for copy in vectors_out + points_out + lists_out + hv_out + hs_out + a_out + x_out + c_out:
         copy.wait_send()
@@ -334,7 +362,6 @@
         leaves, leaf_pts, rank = bases.shape
         cols = vectors.shape[1]
         features = points.shape[1]
-        vt = jnp.transpose(vectors.reshape(leaves, leaf_pts, cols), (0, 2, 1))
         anywhere = pl.BlockSpec(memory_space=pl.ANY)
         vmem = pl.BlockSpec(memory_space=pltpu.VMEM)
         smem = pl.BlockSpec(memory_space=pltpu.SMEM)
@@ -342,17 +369,18 @@
         wide = ydim * cols
         outT = pl.pallas_call(
             functools.partial(kernel, (zdim, xdim, ydim)),
-            out_shape=jax.ShapeDtypeStruct((leaves, cols, leaf_pts), F32),
+            out_shape=jax.ShapeDtypeStruct((cols, leaves * leaf_pts), F32),
             in_specs=[anywhere] * 6 + [smem, smem, vmem],
             out_specs=vmem,
             scratch_shapes=[
+                pltpu.VMEM((features, leaves * leaf_pts), BF16),
                 pltpu.VMEM((leaves, leaf_pts, features), BF16),
-                pltpu.VMEM((2, leaf_pts, features), BF16),
-                pltpu.VMEM((ydim, leaves, cols, leaf_pts), BF16),
+                pltpu.VMEM((2, features, leaf_pts), BF16),
+                pltpu.VMEM((ydim, cols, leaves * leaf_pts), BF16),
                 pltpu.VMEM((2, ydim, cols, leaf_pts), BF16),
                 pltpu.VMEM((2,) + near_lists.shape, jnp.int32),
                 pltpu.VMEM((3, leaves, 128), F32),
-                pltpu.VMEM(bases.shape, F32),
+                pltpu.VMEM((leaves, rank, leaf_pts), F32),
                 pltpu.VMEM((leaves * 8, rank, rank), F32),
                 pltpu.VMEM(transfer.shape, F32),
                 pltpu.VMEM((leaves * 4, rank, rank), F32),
@@ -374,7 +402,7 @@
                 dma((2,)), dma((2,)),
                 dma((2,)), dma((2,)),
                 dma((zdim,)), dma((zdim,)),
-                dma((zdim, xdim - 1)), dma((zdim, xdim - 1)),
+                dma((zdim, 3)), dma((zdim, 3)),
                 dma((xdim,)), dma((xdim,)),
                 dma((2,)), dma((2,)),
                 dma((ydim - 1,)), dma((ydim - 1,)),
@@ -383,9 +411,9 @@
                 collective_id=0, has_side_effects=True, vmem_limit_bytes=56 * 1024 * 1024
             ),
         )(
-            points.reshape(leaves, leaf_pts, features),
-            vt,
-            bases,
+            points.T,
+            vectors.T,
+            jnp.transpose(bases, (0, 2, 1)),
             leaf_coupling.reshape(-1, rank, rank),
             transfer,
             up_coupling.reshape(-1, rank, rank),
@@ -393,7 +421,7 @@
             far_up,
             near_lists,
         )
-        return jnp.transpose(outT, (0, 2, 1)).reshape(leaves * leaf_pts, cols)
+        return outT.T
 
     return jax.shard_map(
         local,

time: 60.6 us -> 51.2 us (0.84); the launches traced: 60.3 us -> 50.3 us
  local copies, waits for them, and re-layouts: 11.6 us -> 1.67 us
    unnamed x2 -> x1, local copies, waits for them, and re-layouts: 8.32 us -> 1.67 us
    reshape x2 -> x0, local copies, waits for them, and re-layouts: 3.24 us -> none  [the longest x1 1.67 us: local(): return jnp.transpose(outT, (0, 2, 1)).reshape(leaves * leaf_pts, cols)]
where the time goes in v2:
time: 51.2 us; the launch traced here: 50.3 us
  Pallas kernels  48.6 us (95%)
  local copies, waits for them, and re-layouts  1.67 us (3%)
    pallas_call x1, Pallas kernels, local(): pl.pallas_call(functools.partial(kernel, (zdim, xdim, ydim)), out_shape=j...  48.6 us
    unnamed x1, local copies, waits for them, and re-layouts  1.67 us

profile of v2, /device:TPU:1, one launch (start us, length us, event | category | flops | bytes accessed | tf_op | source)
XLA Modules:
  0.0 50.3 jit_solution(2254632969953939243)
XLA Ops:
  0.0 48.6 %shard_map.91 = f32[32,2048]{1,0:T(8,128)} custom-call(bf16[784,2048]{1,0:T(8,128)(2,1)} %bitcast.6, bf16[32,2048]{1,0:T(8,128)(2,1)} %bitcast.11, f32[8,64,256]{2,1,0:T(8,128)} %bitcast.10, f32[64,64,64]{2,1,0:T(8,128)} %bitcast.7, f32[8,64,64]{2,1,0:T(8,128)} %tr.1, f32[32,64,64]{2,1,0:T(8,128)} %bitcast.8, s32[8,8]{1,0:T(8,128)} %fl.1, s32[4,8]{1,0:T(4,128)} %fu.1, ...), custom_call_target="tpu_custom_call" | custom-call | tf_op jit(solution)/shard_map/pallas_call | solution.py:370
  48.6 1.7 %copy.11 = f32[2048,32]{0,1:T(8,128)} copy(f32[2048,32]{0,1:T(8,128)} %bitcast.9) | data formatting | bytes 524288

commit v3 on v2

--- a/solution.py
+++ b/solution.py
@@ -30,7 +30,7 @@
     pts, vt, bases, lc, tr, uc, fl, fu, nl,
     out,
     pt, pv, hp, vall, hv, nlr, masks, bv, lv, tv, uv, gat, wl, wu, halves,
-    ncol, nrow, acc, hacc, hsend, hres, asend, arecv,
+    ncol, nrow, tiles, acc, hacc, hsend, hres, asend, arecv,
     lsem, hp_s, hp_r, v_s, v_r, nl_s, nl_r, hv_s, hv_r, z_s, z_r, x_s, x_r, c_s, c_r, hs_s, hs_r, a_s, a_r,
 ):
     zdim, xdim, ydim = dims
@@ -58,8 +58,10 @@
     scale = math.log2(math.e) / features
 
     barrier = pltpu.get_barrier_semaphore()
-    partners = [(nxt, r), (prv, r)]
-    partners += [(d, lax.rem(r + j, ydim)) for j in range(1, ydim)]
+    rhs_at = [lax.rem(r + j, ydim) for j in range(ydim)]
+    rhs_from = [lax.rem(r + ydim - j, ydim) for j in range(ydim)]
+    partners = [(side, to) for side in (nxt, prv) for to in rhs_at]
+    partners += [(d, to) for to in rhs_at[1:]]
     partners += [(leaf_at(lax.rem(z + s, zdim), x, core), r) for s in range(1, zdim)]
     right, left = lax.rem(x + 1, xdim), lax.rem(x + xdim - 1, xdim)
     across = lax.rem(x + 2, xdim)
@@ -94,9 +96,16 @@
         rc(nl, nlr.at[1], nl_s.at[1], nl_r.at[1], nxt, r),
     ]
     vectors_out = [
-        rc(vt, vall.at[r], v_s.at[j - 1], v_r.at[j - 1], d, lax.rem(r + j, ydim)) for j in range(1, ydim)
+        rc(vt, vall.at[r], v_s.at[j - 1], v_r.at[j - 1], d, rhs_at[j]) for j in range(1, ydim)
     ]
-    for copy in vectors_out + points_out + lists_out:
+    hv_out = []
+    for j in range(ydim):
+        to = rhs_at[j]
+        hv_out += [
+            rc(vt.at[:, block_of(to)], hv.at[0, r], hv_s.at[0, j], hv_r.at[0, j], prv, to),
+            rc(vt.at[:, block_of(half_leaves + to)], hv.at[1, r], hv_s.at[1, j], hv_r.at[1, j], nxt, to),
+        ]
+    for copy in vectors_out + points_out + hv_out + lists_out:
         copy.start()
 
     loads[0].wait()
@@ -177,31 +186,32 @@
             rc(block, block, z_s.at[s], z_r.at[s], d, r).wait_recv()
         x_send(s, x, 0, right)
         x_send(s, x, 1, left)
+        to_sibling(s, x, 3)
+
+    c_out = []
+
+    def to_sibling(s, column, kind):
+        block = gat.at[lax.rem(z + zdim - s, zdim), column, core]
+        copy = rc(block, block, c_s.at[s, kind], c_r.at[s, kind], leaf_at(z, x, 1 - core), r)
+        copy.start()
+        c_out.append(copy)
 
     def relay(m):
         s = steps[m]
         if m % 2 == 0:
             x_wait(s, left, 0)
             x_send(s, left, 2, right)
+            to_sibling(s, left, 0)
         else:
             x_wait(s, right, 1)
             x_send(s, right, 2, left)
+            to_sibling(s, right, 1)
 
     forward(0)
     for i in range(leaves):
         acc[i] = jnp.zeros((ydim, cols, leaf_pts), F32)
     hacc[...] = jnp.zeros((2, ydim * cols, leaf_pts), F32)
 
-    for j in range(1, ydim):
-        source = lax.rem(r + ydim - j, ydim)
-        rc(vt, vall.at[source], v_s.at[j - 1], v_r.at[j - 1], d, r).wait_recv()
-    hv_out = [
-        rc(vall.at[:, :, block_of(r)], hv.at[0], hv_s.at[0], hv_r.at[0], prv, r),
-        rc(vall.at[:, :, block_of(half_leaves + r)], hv.at[1], hv_s.at[1], hv_r.at[1], nxt, r),
-    ]
-    for copy in hv_out:
-        copy.start()
-
     lane1 = lax.broadcasted_iota(jnp.int32, (1, 128), 1)
 
     def mask_at(which, row, w):
@@ -218,40 +228,43 @@
     def add(i, value):
         acc[i] = acc[i] + value.reshape(ydim, cols, leaf_pts)
 
-    def own_pair(t):
-        shift = t // 2
+    def pair(t):
         a = 2 * r + t % 2 if t < leaves else r
-        b = lax.rem(a + shift, leaves)
-        tile = tile_of(pv[a], pt[:, block_of(b)], a, b)
+        return a, lax.rem(a + t // 2, leaves)
+
+    def own_tile(t):
+        a, b = pair(t)
+        tiles[t] = tile_of(pv[a], pt[:, block_of(b)], a, b)
+
+    def own_products(t):
+        a, b = pair(t)
         vb = vall[:, :, block_of(b)].reshape(wide)
-        add(a, mm(vb * mask_at(2, a, leaves + b), tile, NT))
-        if shift:
+        add(a, mm(vb * mask_at(2, a, leaves + b), tiles[t], NT))
+        if t // 2:
             va = vall[:, :, block_of(a)].reshape(wide)
-            add(b, mm(va * mask_at(2, b, leaves + a), tile, NN))
+            add(b, mm(va * mask_at(2, b, leaves + a), tiles[t], NN))
 
     for i in range(leaves):
         pv[i] = jnp.transpose(pt[:, block_of(i)])
+    at = {(0, 4): 0, (0, 6): 1, (0, 8): 2, (1, 1): 3, (1, 3): 4, (1, 5): 5, (1, 7): 6}
     for t in range(leaves + 1):
-        own_pair(t)
-        if t < zdim - 1:
-            forward(order[t])
-        if t >= 3:
-            relay(t - 3)
-
-    c_out = []
-
-    def to_sibling(m, j):
-        column = gat.at[:, j, core]
-        copy = rc(column, column, c_s.at[m], c_r.at[m], leaf_at(z, x, 1 - core), r)
-        copy.start()
-        c_out.append(copy)
-
-    to_sibling(0, x)
+        own_tile(t)
+        if (0, t) in at:
+            forward(order[at[0, t]])
+    for j in range(1, ydim):
+        rc(vt, vall.at[rhs_from[j]], v_s.at[j - 1], v_r.at[j - 1], d, r).wait_recv()
+    for t in range(leaves + 1):
+        own_products(t)
+        if (1, t) in at:
+            forward(order[at[1, t]])
+        if t == leaves:
+            relay(0)
 
     for h in range(2):
         points_out[h].wait_recv()
         lists_out[h].wait_recv()
-        rc(vall.at[:, :, block_of(r)], hv.at[h], hv_s.at[h], hv_r.at[h], d, r).wait_recv()
+        for j in range(ydim):
+            rc(vt.at[:, block_of(r)], hv.at[h, rhs_from[j]], hv_s.at[h, j], hv_r.at[h, j], d, r).wait_recv()
         masks[h] = mask_of(nlr[h])
         norms(leaves + h, hp[h])
 
@@ -267,9 +280,13 @@
 
     for p in range(leaves + 1):
         halo_pair(p, 0)
-        if p < 2:
-            relay(6 + p)
+        if p in (2, 5, 8):
+            relay(1 + p // 3)
     hsend[...] = hacc[...].reshape(2, ydim, cols, leaf_pts).astype(BF16)
+
+    for j in (2, 1, 3):
+        for i in range(leaves):
+            asend[j - 1, i] = acc[i, rhs_at[j]].astype(BF16)
 
     loads[4].wait()
     loads[5].wait()
@@ -280,47 +297,47 @@
             dst[i, :, 2 * rank * k : 2 * rank * (k + 1)] = jnp.concatenate([w, w], axis=1).astype(BF16)
 
     widen(wu, uv, 0)
-    hs_out = [
-        rc(hsend.at[0], hres.at[0], hs_s.at[0], hs_r.at[0], nxt, r),
-        rc(hsend.at[1], hres.at[1], hs_s.at[1], hs_r.at[1], prv, r),
+    a_out = [
+        rc(asend.at[j - 1], arecv.at[j - 1], a_s.at[j - 1], a_r.at[j - 1], d, rhs_at[j]) for j in (2, 1, 3)
     ]
-    for copy in hs_out:
+    hs_out = []
+    for j in range(ydim):
+        to = rhs_at[j]
+        hs_out += [
+            rc(hsend.at[0, to], hres.at[0, r], hs_s.at[0, j], hs_r.at[0, j], nxt, to),
+            rc(hsend.at[1, to], hres.at[1, r], hs_s.at[1, j], hs_r.at[1, j], prv, to),
+        ]
+    for copy in a_out + hs_out:
         copy.start()
+    relay(4)
     for q in range(1, leaves // 2):
         widen(wu, uv, q)
-
-    for h in range(2):
-        hs_out[h].wait_recv()
-        i = r + half_leaves * h
-        acc[i] = acc[i] + hres[h].astype(F32)
-    for j in range(1, ydim):
-        target = lax.rem(r + j, ydim)
-        for i in range(leaves):
-            asend[j - 1, i] = acc[i, target].astype(BF16)
-    widen(wl, lv, 0)
-    a_out = [
-        rc(asend.at[j - 1], arecv.at[j - 1], a_s.at[j - 1], a_r.at[j - 1], d, lax.rem(r + j, ydim))
-        for j in range(1, ydim)
-    ]
-    for copy in a_out:
-        copy.start()
-    for i in range(1, leaves):
+    relay(5)
+    for i in range(leaves // 2):
         widen(wl, lv, i)
-
-    for m in range(1, zdim, 2):
-        x_wait(steps[m], left, 0)
-    to_sibling(1, left)
-    for m in range(0, zdim, 2):
-        x_wait(steps[m], right, 1)
-    to_sibling(2, right)
+    relay(6)
+    for i in range(leaves // 2, leaves):
+        widen(wl, lv, i)
+    relay(7)
+
     for m in range(zdim):
+        if m % 2:
+            x_wait(steps[m], left, 0)
+            to_sibling(steps[m], left, 0)
+        else:
+            x_wait(steps[m], right, 1)
+            to_sibling(steps[m], right, 1)
         x_wait(steps[m], across, 2)
-    to_sibling(3, across)
+        to_sibling(steps[m], across, 2)
     for j in range(ydim - 1):
         a_out[j].wait_recv()
-    for m, j in enumerate((x, left, right, across)):
-        column = gat.at[:, j, 1 - core]
-        rc(column, column, c_s.at[m], c_r.at[m], d, r).wait_recv()
+    for h in range(2):
+        for j in range(ydim):
+            rc(hsend.at[h, r], hres.at[h, rhs_from[j]], hs_s.at[h, j], hs_r.at[h, j], d, r).wait_recv()
+    for s in steps:
+        for kind, column in enumerate((left, right, across, x)):
+            block = gat.at[lax.rem(z + zdim - s, zdim), column, 1 - core]
+            rc(block, block, c_s.at[s, kind], c_r.at[s, kind], d, r).wait_recv()
 
     def gathered(index, per_device, first):
         device = lax.div(index, per_device)
@@ -341,7 +358,7 @@
             fh, fo = split(field)
             bh, bl = split(bv[i])
             far = mm(fh, bh) + (mm(fo, bh) + mm(fh, bl))
-            near = acc[i, r]
+            near = acc[i, r] + hres[i // half_leaves, i % half_leaves].astype(F32)
             for j in range(ydim - 1):
                 near = near + arecv[j, i].astype(F32)
             out[:, block_of(i)] = near + far + RIDGE * vall[r, :, block_of(i)].astype(F32)
@@ -390,6 +407,7 @@
                 pltpu.VMEM((2, cols, 2 * rank), BF16),
                 pltpu.VMEM((leaves + 2, leaf_pts, 128), F32),
                 pltpu.VMEM((leaves + 2, 1, leaf_pts), F32),
+                pltpu.VMEM((leaves + 1, leaf_pts, leaf_pts), BF16),
                 pltpu.VMEM((leaves, ydim, cols, leaf_pts), F32),
                 pltpu.VMEM((2, wide, leaf_pts), F32),
                 pltpu.VMEM((2, ydim, cols, leaf_pts), BF16),
@@ -400,11 +418,11 @@
                 dma((2,)), dma((2,)),
                 dma((ydim - 1,)), dma((ydim - 1,)),
                 dma((2,)), dma((2,)),
-                dma((2,)), dma((2,)),
+                dma((2, ydim)), dma((2, ydim)),
                 dma((zdim,)), dma((zdim,)),
                 dma((zdim, 3)), dma((zdim, 3)),
-                dma((xdim,)), dma((xdim,)),
-                dma((2,)), dma((2,)),
+                dma((zdim, 4)), dma((zdim, 4)),
+                dma((2, ydim)), dma((2, ydim)),
                 dma((ydim - 1,)), dma((ydim - 1,)),
             ],
             compiler_params=pltpu.CompilerParams(

time: 51.2 us -> 45.6 us (0.89); the launches traced: 50.3 us -> 45.4 us
  Pallas kernels: 48.6 us -> 43.8 us
    pallas_call x1, Pallas kernels: 48.6 us -> 43.8 us  [local(): pl.pallas_call(functools.partial(kernel, (zdim, xdim, ydim)), out_shape=j...]
where the time goes in v3:
time: 45.6 us; the launch traced here: 45.4 us
  Pallas kernels  43.8 us (96%)
  local copies, waits for them, and re-layouts  1.67 us (4%)
    pallas_call x1, Pallas kernels, local(): pl.pallas_call(functools.partial(kernel, (zdim, xdim, ydim)), out_shape=j...  43.8 us
    unnamed x1, local copies, waits for them, and re-layouts  1.67 us

profile of v3, /device:TPU:1, one launch (start us, length us, event | category | flops | bytes accessed | tf_op | source)
XLA Modules:
  0.0 45.4 jit_solution(17031384999470623345)
XLA Ops:
  0.0 43.8 %shard_map.91 = f32[32,2048]{1,0:T(8,128)} custom-call(bf16[784,2048]{1,0:T(8,128)(2,1)} %bitcast.6, bf16[32,2048]{1,0:T(8,128)(2,1)} %bitcast.11, f32[8,64,256]{2,1,0:T(8,128)} %bitcast.10, f32[64,64,64]{2,1,0:T(8,128)} %bitcast.7, f32[8,64,64]{2,1,0:T(8,128)} %tr.1, f32[32,64,64]{2,1,0:T(8,128)} %bitcast.8, s32[8,8]{1,0:T(8,128)} %fl.1, s32[4,8]{1,0:T(4,128)} %fu.1, ...), custom_call_target="tpu_custom_call" | custom-call | tf_op jit(solution)/shard_map/pallas_call | solution.py:387
  43.8 1.7 %copy.11 = f32[2048,32]{0,1:T(8,128)} copy(f32[2048,32]{0,1:T(8,128)} %bitcast.9) | data formatting | bytes 524288

commit v4 on v3

--- a/solution.py
+++ b/solution.py
@@ -60,9 +60,10 @@
     barrier = pltpu.get_barrier_semaphore()
     rhs_at = [lax.rem(r + j, ydim) for j in range(ydim)]
     rhs_from = [lax.rem(r + ydim - j, ydim) for j in range(ydim)]
-    partners = [(side, to) for side in (nxt, prv) for to in rhs_at]
+    partners = [(nxt, r), (prv, r)]
     partners += [(d, to) for to in rhs_at[1:]]
-    partners += [(leaf_at(lax.rem(z + s, zdim), x, core), r) for s in range(1, zdim)]
+    up, down = lax.rem(z + 1, zdim), lax.rem(z + zdim - 1, zdim)
+    partners += [(leaf_at(up, x, core), r), (leaf_at(down, x, core), r)]
     right, left = lax.rem(x + 1, xdim), lax.rem(x + xdim - 1, xdim)
     across = lax.rem(x + 2, xdim)
     partners += [(leaf_at(z, right, core), r), (leaf_at(z, left, core), r)]
@@ -75,16 +76,16 @@
         pltpu.make_async_copy(bases, bv, lsem.at[1]),
         pltpu.make_async_copy(tr, tv, lsem.at[2]),
         pltpu.make_async_copy(pts, pt, lsem.at[3]),
-        pltpu.make_async_copy(lc, lv, lsem.at[4]),
-        pltpu.make_async_copy(uc, uv, lsem.at[5]),
+        pltpu.make_async_copy(uc, uv, lsem.at[4]),
+        pltpu.make_async_copy(lc, lv, lsem.at[5]),
     ]
     for copy in loads:
         copy.start()
 
-    pl.semaphore_wait(barrier, len(partners))
-
     def block_of(i):
         return pl.ds(pl.multiple_of(i * leaf_pts, leaf_pts), leaf_pts)
+
+    pl.semaphore_wait(barrier, len(partners))
 
     half_leaves = leaves // 2
     points_out = [
@@ -98,14 +99,7 @@
     vectors_out = [
         rc(vt, vall.at[r], v_s.at[j - 1], v_r.at[j - 1], d, rhs_at[j]) for j in range(1, ydim)
     ]
-    hv_out = []
-    for j in range(ydim):
-        to = rhs_at[j]
-        hv_out += [
-            rc(vt.at[:, block_of(to)], hv.at[0, r], hv_s.at[0, j], hv_r.at[0, j], prv, to),
-            rc(vt.at[:, block_of(half_leaves + to)], hv.at[1, r], hv_s.at[1, j], hv_r.at[1, j], nxt, to),
-        ]
-    for copy in vectors_out + points_out + hv_out + lists_out:
+    for copy in vectors_out + points_out + lists_out:
         copy.start()
 
     loads[0].wait()
@@ -144,31 +138,21 @@
     halves[0] = jnp.where(lane_half < rank, 1.0, 0.0).astype(BF16)
     halves[1] = jnp.where(lane_half < rank, 0.0, 1.0).astype(BF16)
 
-    loads[3].wait()
-
-    def norms(index, block):
-        wide = block.astype(F32)
-        row = jnp.sum(wide * wide, axis=0, keepdims=True) * (-scale)
-        nrow[index] = row
-        if index < leaves:
-            ncol[index] = jnp.transpose(jnp.broadcast_to(row, (128, leaf_pts)))
-
-    for i in range(leaves):
-        norms(i, pt[:, block_of(i)])
-
-    order = sorted(range(1, zdim), key=lambda s: (min(s, zdim - s), s))
-    z_out = {
-        s: rc(
-            gat.at[z, x, core], gat.at[z, x, core], z_s.at[s], z_r.at[s],
-            leaf_at(lax.rem(z + s, zdim), x, core), r,
-        )
-        for s in order
-    }
-    for s in order:
-        z_out[s].start()
+    top = zdim // 2
+    z_out = []
+
+    def z_send(s, to):
+        block = gat.at[lax.rem(z + zdim - s, zdim), x, core]
+        target = up if to <= top else down
+        copy = rc(block, block, z_s.at[to], z_r.at[to], leaf_at(target, x, core), r)
+        copy.start()
+        z_out.append(copy)
+
+    z_send(0, 1)
+    z_send(0, zdim - 1)
 
     x_out = []
-    steps = [0] + order
+    steps = sorted(range(zdim), key=lambda s: (min(s, zdim - s), s))
 
     def x_send(s, column, kind, target):
         block = gat.at[lax.rem(z + zdim - s, zdim), column, core]
@@ -180,10 +164,15 @@
         block = gat.at[lax.rem(z + zdim - s, zdim), column, core]
         rc(block, block, x_s.at[s, kind], x_r.at[s, kind], d, r).wait_recv()
 
-    def forward(s):
-        if s:
-            block = gat.at[lax.rem(z + zdim - s, zdim), x, core]
-            rc(block, block, z_s.at[s], z_r.at[s], d, r).wait_recv()
+    def z_forward(s):
+        block = gat.at[lax.rem(z + zdim - s, zdim), x, core]
+        rc(block, block, z_s.at[s], z_r.at[s], d, r).wait_recv()
+        if s < top:
+            z_send(s, s + 1)
+        elif s > top + 1:
+            z_send(s, s - 1)
+
+    def x_forward(s):
         x_send(s, x, 0, right)
         x_send(s, x, 1, left)
         to_sibling(s, x, 3)
@@ -207,7 +196,18 @@
             x_send(s, right, 2, left)
             to_sibling(s, right, 1)
 
-    forward(0)
+    loads[3].wait()
+
+    def norms(index, block):
+        wide = block.astype(F32)
+        row = jnp.sum(wide * wide, axis=0, keepdims=True) * (-scale)
+        nrow[index] = row
+        if index < leaves:
+            ncol[index] = jnp.transpose(jnp.broadcast_to(row, (128, leaf_pts)))
+
+    for i in range(leaves):
+        norms(i, pt[:, block_of(i)])
+
     for i in range(leaves):
         acc[i] = jnp.zeros((ydim, cols, leaf_pts), F32)
     hacc[...] = jnp.zeros((2, ydim * cols, leaf_pts), F32)
@@ -246,78 +246,122 @@
 
     for i in range(leaves):
         pv[i] = jnp.transpose(pt[:, block_of(i)])
-    at = {(0, 4): 0, (0, 6): 1, (0, 8): 2, (1, 1): 3, (1, 3): 4, (1, 5): 5, (1, 7): 6}
     for t in range(leaves + 1):
         own_tile(t)
-        if (0, t) in at:
-            forward(order[at[0, t]])
-    for j in range(1, ydim):
-        rc(vt, vall.at[rhs_from[j]], v_s.at[j - 1], v_r.at[j - 1], d, r).wait_recv()
-    for t in range(leaves + 1):
-        own_products(t)
-        if (1, t) in at:
-            forward(order[at[1, t]])
-        if t == leaves:
-            relay(0)
-
-    for h in range(2):
-        points_out[h].wait_recv()
-        lists_out[h].wait_recv()
-        for j in range(ydim):
-            rc(vt.at[:, block_of(r)], hv.at[h, rhs_from[j]], hv_s.at[h, j], hv_r.at[h, j], d, r).wait_recv()
-        masks[h] = mask_of(nlr[h])
-        norms(leaves + h, hp[h])
-
-    def halo_pair(p, carry):
-        side = lax.div(p + r, leaves)
-        o = p + r - half_leaves * side
-        tile = tile_of(pv[o], hp[side], o, leaves + side)
-        vh = hv[side].reshape(wide)
-        add(o, mm(vh * mask_at(2, o, 2 * leaves + r - (leaves + half_leaves) * side), tile, NT))
-        vo = vall[:, :, block_of(o)].reshape(wide)
-        hacc[side] = hacc[side] + mm(vo * mask_at(side, r + half_leaves * side, leaves + o), tile, NN)
-        return carry
-
-    for p in range(leaves + 1):
-        halo_pair(p, 0)
-        if p in (2, 5, 8):
-            relay(1 + p // 3)
-    hsend[...] = hacc[...].reshape(2, ydim, cols, leaf_pts).astype(BF16)
-
-    for j in (2, 1, 3):
-        for i in range(leaves):
-            asend[j - 1, i] = acc[i, rhs_at[j]].astype(BF16)
-
-    loads[4].wait()
-    loads[5].wait()
+        if t == 5:
+            z_forward(steps[1])
+            z_forward(steps[2])
+    for m in range(3):
+        x_forward(steps[m])
 
     def widen(dst, src, i):
         for k in range(8):
             w = src[i * 8 + k]
             dst[i, :, 2 * rank * k : 2 * rank * (k + 1)] = jnp.concatenate([w, w], axis=1).astype(BF16)
 
-    widen(wu, uv, 0)
-    a_out = [
-        rc(asend.at[j - 1], arecv.at[j - 1], a_s.at[j - 1], a_r.at[j - 1], d, rhs_at[j]) for j in (2, 1, 3)
+    loads[4].wait()
+    for q in range(leaves // 2):
+        widen(wu, uv, q)
+    z_forward(steps[3])
+    z_forward(steps[4])
+
+    for h in range(2):
+        points_out[h].wait_recv()
+        norms(leaves + h, hp[h])
+
+    def halo_of(p):
+        side = lax.div(p + r, leaves)
+        return side, p + r - half_leaves * side
+
+    for p in range(leaves + 1):
+        side, o = halo_of(p)
+        tiles[leaves + 1 + p] = tile_of(pv[o], hp[side], o, leaves + side)
+        if p == 3:
+            x_forward(steps[3])
+            x_forward(steps[4])
+        if p == 5:
+            relay(0)
+
+    for h in range(2):
+        lists_out[h].wait_recv()
+        masks[h] = mask_of(nlr[h])
+    z_forward(steps[5])
+    z_forward(steps[6])
+    x_forward(steps[5])
+    x_forward(steps[6])
+    for j in range(1, ydim):
+        rc(vt, vall.at[rhs_from[j]], v_s.at[j - 1], v_r.at[j - 1], d, r).wait_recv()
+    hv_out = [
+        rc(vall.at[:, :, block_of(r)], hv.at[0], hv_s.at[0], hv_r.at[0], prv, r),
+        rc(vall.at[:, :, block_of(half_leaves + r)], hv.at[1], hv_s.at[1], hv_r.at[1], nxt, r),
     ]
-    hs_out = []
-    for j in range(ydim):
-        to = rhs_at[j]
-        hs_out += [
-            rc(hsend.at[0, to], hres.at[0, r], hs_s.at[0, j], hs_r.at[0, j], nxt, to),
-            rc(hsend.at[1, to], hres.at[1, r], hs_s.at[1, j], hs_r.at[1, j], prv, to),
-        ]
-    for copy in a_out + hs_out:
-        copy.start()
+    for copy in hv_out:
+        copy.start()
+
+    def halo_in(p):
+        side, o = halo_of(p)
+        vh = hv[side].reshape(wide)
+        add(o, mm(vh * mask_at(2, o, 2 * leaves + r - (leaves + half_leaves) * side), tiles[leaves + 1 + p], NT))
+
+    def halo_back(p):
+        side, o = halo_of(p)
+        vo = vall[:, :, block_of(o)].reshape(wide)
+        hacc[side] = hacc[side] + mm(vo * mask_at(side, r + half_leaves * side, leaves + o), tiles[leaves + 1 + p])
+
+    for p in range(leaves + 1):
+        halo_back(p)
+    hsend[...] = hacc[...].reshape(2, ydim, cols, leaf_pts).astype(BF16)
+    own_products(0)
+    own_products(1)
+    hs_out = [
+        rc(hsend.at[0], hres.at[0], hs_s.at[0], hs_r.at[0], nxt, r),
+        rc(hsend.at[1], hres.at[1], hs_s.at[1], hs_r.at[1], prv, r),
+    ]
+    for copy in hs_out:
+        copy.start()
+    relay(1)
+    relay(2)
+    for t in range(2, leaves + 1):
+        own_products(t)
+    z_forward(steps[7])
+    x_forward(steps[7])
+    for h in range(2):
+        hv_out[h].wait_recv()
+
+    a_out = []
+
+    def wave(w):
+        hs_out[w].wait_recv()
+        acc[r + half_leaves * w] = acc[r + half_leaves * w] + hres[w].astype(F32)
+        for j in (2, 1, 3):
+            for i in range(half_leaves):
+                asend[j - 1, w, i] = acc[half_leaves * w + i, rhs_at[j]].astype(BF16)
+
+    def wave_start(w):
+        for j in (2, 1, 3):
+            copy = rc(
+                asend.at[j - 1, w], arecv.at[j - 1, w], a_s.at[j - 1, w], a_r.at[j - 1, w], d, rhs_at[j]
+            )
+            copy.start()
+            a_out.append(copy)
+
+    for p in range(half_leaves):
+        halo_in(p)
+    wave(0)
+    halo_in(half_leaves)
+    wave_start(0)
+    for p in range(half_leaves + 1, leaves + 1):
+        halo_in(p)
+    wave(1)
+    loads[5].wait()
+    widen(wl, lv, 0)
+    wave_start(1)
+    relay(3)
     relay(4)
-    for q in range(1, leaves // 2):
-        widen(wu, uv, q)
+    for i in range(1, leaves):
+        widen(wl, lv, i)
     relay(5)
-    for i in range(leaves // 2):
-        widen(wl, lv, i)
     relay(6)
-    for i in range(leaves // 2, leaves):
-        widen(wl, lv, i)
     relay(7)
 
     for m in range(zdim):
@@ -329,11 +373,14 @@
             to_sibling(steps[m], right, 1)
         x_wait(steps[m], across, 2)
         to_sibling(steps[m], across, 2)
-    for j in range(ydim - 1):
-        a_out[j].wait_recv()
-    for h in range(2):
-        for j in range(ydim):
-            rc(hsend.at[h, r], hres.at[h, rhs_from[j]], hs_s.at[h, j], hs_r.at[h, j], d, r).wait_recv()
+    for copy in a_out:
+        copy.wait_recv()
+    for i in range(leaves):
+        w, e = i // half_leaves, i % half_leaves
+        near = acc[i, r]
+        for j in range(ydim - 1):
+            near = near + arecv[j, w, e].astype(F32)
+        out[:, block_of(i)] = near + RIDGE * vall[r, :, block_of(i)].astype(F32)
     for s in steps:
         for kind, column in enumerate((left, right, across, x)):
             block = gat.at[lax.rem(z + zdim - s, zdim), column, 1 - core]
@@ -358,15 +405,10 @@
             fh, fo = split(field)
             bh, bl = split(bv[i])
             far = mm(fh, bh) + (mm(fo, bh) + mm(fh, bl))
-            near = acc[i, r] + hres[i // half_leaves, i % half_leaves].astype(F32)
-            for j in range(ydim - 1):
-                near = near + arecv[j, i].astype(F32)
-            out[:, block_of(i)] = near + far + RIDGE * vall[r, :, block_of(i)].astype(F32)
-
-    for copy in vectors_out + points_out + lists_out + hv_out + hs_out + a_out + x_out + c_out:
+            out[:, block_of(i)] = out[:, block_of(i)] + far
+
+    for copy in vectors_out + points_out + lists_out + hv_out + hs_out + a_out + x_out + c_out + z_out:
         copy.wait_send()
-    for s in order:
-        z_out[s].wait_send()
 
 
 def solution(mesh):
@@ -407,23 +449,23 @@
                 pltpu.VMEM((2, cols, 2 * rank), BF16),
                 pltpu.VMEM((leaves + 2, leaf_pts, 128), F32),
                 pltpu.VMEM((leaves + 2, 1, leaf_pts), F32),
-                pltpu.VMEM((leaves + 1, leaf_pts, leaf_pts), BF16),
+                pltpu.VMEM((2 * leaves + 2, leaf_pts, leaf_pts), BF16),
                 pltpu.VMEM((leaves, ydim, cols, leaf_pts), F32),
                 pltpu.VMEM((2, wide, leaf_pts), F32),
                 pltpu.VMEM((2, ydim, cols, leaf_pts), BF16),
                 pltpu.VMEM((2, ydim, cols, leaf_pts), BF16),
-                pltpu.VMEM((ydim - 1, leaves, cols, leaf_pts), BF16),
-                pltpu.VMEM((ydim - 1, leaves, cols, leaf_pts), BF16),
+                pltpu.VMEM((ydim - 1, 2, leaves // 2, cols, leaf_pts), BF16),
+                pltpu.VMEM((ydim - 1, 2, leaves // 2, cols, leaf_pts), BF16),
                 dma((6,)),
                 dma((2,)), dma((2,)),
                 dma((ydim - 1,)), dma((ydim - 1,)),
                 dma((2,)), dma((2,)),
-                dma((2, ydim)), dma((2, ydim)),
+                dma((2,)), dma((2,)),
                 dma((zdim,)), dma((zdim,)),
                 dma((zdim, 3)), dma((zdim, 3)),
                 dma((zdim, 4)), dma((zdim, 4)),
-                dma((2, ydim)), dma((2, ydim)),
-                dma((ydim - 1,)), dma((ydim - 1,)),
+                dma((2,)), dma((2,)),
+                dma((ydim - 1, 2)), dma((ydim - 1, 2)),
             ],
             compiler_params=pltpu.CompilerParams(
                 collective_id=0, has_side_effects=True, vmem_limit_bytes=56 * 1024 * 1024

time: 45.6 us -> 41.3 us (0.906)
  Pallas kernels: 43.8 us -> 39.3 us
    pallas_call x1, Pallas kernels: 43.8 us -> 39.3 us  [local(): pl.pallas_call(functools.partial(kernel, (zdim, xdim, ydim)), out_shape=j...]
where the time goes in v4:
time: 41.3 us; the launch traced here: 41 us
  Pallas kernels  39.3 us (95%)
  local copies, waits for them, and re-layouts  1.67 us (4%)
    pallas_call x1, Pallas kernels, local(): pl.pallas_call(functools.partial(kernel, (zdim, xdim, ydim)), out_shape=j...  39.3 us
    unnamed x1, local copies, waits for them, and re-layouts  1.67 us

profile of v4, /device:TPU:1, one launch (start us, length us, event | category | flops | bytes accessed | tf_op | source)
XLA Modules:
  0.0 41.0 jit_solution(9150964813314184514)
XLA Ops:
  0.0 39.3 %shard_map.91 = f32[32,2048]{1,0:T(8,128)} custom-call(bf16[784,2048]{1,0:T(8,128)(2,1)} %bitcast.6, bf16[32,2048]{1,0:T(8,128)(2,1)} %bitcast.11, f32[8,64,256]{2,1,0:T(8,128)} %bitcast.10, f32[64,64,64]{2,1,0:T(8,128)} %bitcast.7, f32[8,64,64]{2,1,0:T(8,128)} %tr.1, f32[32,64,64]{2,1,0:T(8,128)} %bitcast.8, s32[8,8]{1,0:T(8,128)} %fl.1, s32[4,8]{1,0:T(4,128)} %fu.1, ...), custom_call_target="tpu_custom_call" | custom-call | tf_op jit(solution)/shard_map/pallas_call | solution.py:429
  39.3 1.7 %copy.11 = f32[2048,32]{0,1:T(8,128)} copy(f32[2048,32]{0,1:T(8,128)} %bitcast.9) | data formatting | bytes 524288

commit v5 on v4

--- a/solution.py
+++ b/solution.py
@@ -27,11 +27,11 @@
 
 def kernel(
     dims,
-    pts, vt, bases, lc, tr, uc, fl, fu, nl,
+    pts, vt, bases, lc, tr, uc, fl_in, fu_in, nl,
     out,
     pt, pv, hp, vall, hv, nlr, masks, bv, lv, tv, uv, gat, wl, wu, halves,
     ncol, nrow, tiles, acc, hacc, hsend, hres, asend, arecv,
-    lsem, hp_s, hp_r, v_s, v_r, nl_s, nl_r, hv_s, hv_r, z_s, z_r, x_s, x_r, c_s, c_r, hs_s, hs_r, a_s, a_r,
+    fl, fu, nlo, lsem, hp_s, hp_r, v_s, v_r, nl_s, nl_r, hv_s, hv_r, z_s, z_r, x_s, x_r, c_s, c_r, hs_s, hs_r, a_s, a_r,
 ):
     zdim, xdim, ydim = dims
     n = zdim * xdim * 2
@@ -78,6 +78,9 @@
         pltpu.make_async_copy(pts, pt, lsem.at[3]),
         pltpu.make_async_copy(uc, uv, lsem.at[4]),
         pltpu.make_async_copy(lc, lv, lsem.at[5]),
+        pltpu.make_async_copy(nl, nlo, lsem.at[6]),
+        pltpu.make_async_copy(fl_in, fl, lsem.at[7]),
+        pltpu.make_async_copy(fu_in, fu, lsem.at[8]),
     ]
     for copy in loads:
         copy.start()
@@ -123,7 +126,8 @@
     for m in range(len(parts) // 2):
         gat[z, x, core, m] = jnp.concatenate(parts[2 * m : 2 * m + 2], axis=1).astype(BF16)
 
-    nl_own = nl[...]
+    loads[6].wait()
+    nl_own = nlo[...]
     lane = lax.broadcasted_iota(jnp.int32, (leaves, 128), 1) + (d - 1) * leaves
 
     def mask_of(lists):
@@ -262,9 +266,6 @@
     loads[4].wait()
     for q in range(leaves // 2):
         widen(wu, uv, q)
-    z_forward(steps[3])
-    z_forward(steps[4])
-
     for h in range(2):
         points_out[h].wait_recv()
         norms(leaves + h, hp[h])
@@ -276,7 +277,9 @@
     for p in range(leaves + 1):
         side, o = halo_of(p)
         tiles[leaves + 1 + p] = tile_of(pv[o], hp[side], o, leaves + side)
-        if p == 3:
+        if p == 2:
+            z_forward(steps[3])
+            z_forward(steps[4])
             x_forward(steps[3])
             x_forward(steps[4])
         if p == 5:
@@ -285,10 +288,6 @@
     for h in range(2):
         lists_out[h].wait_recv()
         masks[h] = mask_of(nlr[h])
-    z_forward(steps[5])
-    z_forward(steps[6])
-    x_forward(steps[5])
-    x_forward(steps[6])
     for j in range(1, ydim):
         rc(vt, vall.at[rhs_from[j]], v_s.at[j - 1], v_r.at[j - 1], d, r).wait_recv()
     hv_out = [
@@ -319,12 +318,14 @@
     ]
     for copy in hs_out:
         copy.start()
+    z_forward(steps[5])
+    z_forward(steps[6])
+    x_forward(steps[5])
+    x_forward(steps[6])
+    for t in range(2, leaves + 1):
+        own_products(t)
     relay(1)
     relay(2)
-    for t in range(2, leaves + 1):
-        own_products(t)
-    z_forward(steps[7])
-    x_forward(steps[7])
     for h in range(2):
         hv_out[h].wait_recv()
 
@@ -350,6 +351,8 @@
     wave(0)
     halo_in(half_leaves)
     wave_start(0)
+    z_forward(steps[7])
+    x_forward(steps[7])
     for p in range(half_leaves + 1, leaves + 1):
         halo_in(p)
     wave(1)
@@ -394,18 +397,27 @@
         ]
         return block * halves[lax.rem(inner, 2)]
 
+    loads[7].wait()
+    loads[8].wait()
+    uppers = []
     for q in range(leaves // 2):
-        left = jnp.concatenate([gathered(fu[q, k], leaves // 2, leaves // 2) for k in range(8)], axis=1)
-        upper = mm(left, wu[q], NT)
-        uh, ul = split(upper)
-        for i in (2 * q, 2 * q + 1):
-            left = jnp.concatenate([gathered(fl[i, k], leaves, 0) for k in range(8)], axis=1)
-            th, tl = split(tv[i])
-            field = mm(left, wl[i], NT) + (mm(uh, th, NT) + mm(ul, th, NT) + mm(uh, tl, NT))
-            fh, fo = split(field)
-            bh, bl = split(bv[i])
-            far = mm(fh, bh) + (mm(fo, bh) + mm(fh, bl))
-            out[:, block_of(i)] = out[:, block_of(i)] + far
+        left_in = jnp.concatenate([gathered(fu[q, k], leaves // 2, leaves // 2) for k in range(8)], axis=1)
+        uppers.append(split(mm(left_in, wu[q], NT)))
+    fields = []
+    for i in range(leaves):
+        left_in = jnp.concatenate([gathered(fl[i, k], leaves, 0) for k in range(8)], axis=1)
+        fields.append(mm(left_in, wl[i], NT))
+    for i in range(leaves):
+        th, tl = split(tv[i])
+        uh, ul = uppers[i // 2]
+        fields[i] = split(fields[i] + (mm(uh, th, NT) + mm(ul, th, NT) + mm(uh, tl, NT)))
+    fars = []
+    for i in range(leaves):
+        fh, fo = fields[i]
+        bh, bl = split(bv[i])
+        fars.append(mm(fh, bh) + (mm(fo, bh) + mm(fh, bl)))
+    for i in range(leaves):
+        out[:, block_of(i)] = out[:, block_of(i)] + fars[i]
 
     for copy in vectors_out + points_out + lists_out + hv_out + hs_out + a_out + x_out + c_out + z_out:
         copy.wait_send()
@@ -423,13 +435,12 @@
         features = points.shape[1]
         anywhere = pl.BlockSpec(memory_space=pl.ANY)
         vmem = pl.BlockSpec(memory_space=pltpu.VMEM)
-        smem = pl.BlockSpec(memory_space=pltpu.SMEM)
         dma = pltpu.SemaphoreType.DMA
         wide = ydim * cols
         outT = pl.pallas_call(
             functools.partial(kernel, (zdim, xdim, ydim)),
-            out_shape=jax.ShapeDtypeStruct((cols, leaves * leaf_pts), F32),
-            in_specs=[anywhere] * 6 + [smem, smem, vmem],
+            out_shape=pltpu.VMEM((cols, leaves * leaf_pts), F32),
+            in_specs=[anywhere] * 9,
             out_specs=vmem,
             scratch_shapes=[
                 pltpu.VMEM((features, leaves * leaf_pts), BF16),
@@ -456,7 +467,10 @@
                 pltpu.VMEM((2, ydim, cols, leaf_pts), BF16),
                 pltpu.VMEM((ydim - 1, 2, leaves // 2, cols, leaf_pts), BF16),
                 pltpu.VMEM((ydim - 1, 2, leaves // 2, cols, leaf_pts), BF16),
-                dma((6,)),
+                pltpu.SMEM(far_leaf.shape, jnp.int32),
+                pltpu.SMEM(far_up.shape, jnp.int32),
+                pltpu.VMEM(near_lists.shape, jnp.int32),
+                dma((9,)),
                 dma((2,)), dma((2,)),
                 dma((ydim - 1,)), dma((ydim - 1,)),
                 dma((2,)), dma((2,)),

time: 41.3 us -> 37.5 us (0.908)
  Pallas kernels: 39.3 us -> 36.5 us
  local copies, waits for them, and re-layouts: 1.67 us -> 0.71 us
    pallas_call x1, Pallas kernels: 39.3 us -> 36.5 us  [local(): pl.pallas_call(functools.partial(kernel, (zdim, xdim, ydim)), out_shape=p...]
    unnamed x1, local copies, waits for them, and re-layouts: 1.67 us -> 0.71 us
where the time goes in v5:
time: 37.5 us; the launch traced here: 37.2 us
  Pallas kernels  36.5 us (97%)
  local copies, waits for them, and re-layouts  0.71 us (2%)
    pallas_call x1, Pallas kernels, local(): pl.pallas_call(functools.partial(kernel, (zdim, xdim, ydim)), out_shape=p...  36.5 us

profile of v5, /device:TPU:1, one launch (start us, length us, event | category | flops | bytes accessed | tf_op | source)
XLA Modules:
  0.0 37.2 jit_solution(4042439797875167305)
XLA Ops:
  0.0 36.5 %shard_map.91 = f32[32,2048]{1,0:T(8,128)S(1)} custom-call(bf16[784,2048]{1,0:T(8,128)(2,1)} %bitcast.7, bf16[32,2048]{1,0:T(8,128)(2,1)} %bitcast.11, f32[8,64,256]{2,1,0:T(8,128)} %bitcast.10, f32[64,64,64]{2,1,0:T(8,128)} %bitcast.8, f32[8,64,64]{2,1,0:T(8,128)} %tr.1, f32[32,64,64]{2,1,0:T(8,128)} %bitcast.9, s32[8,8]{1,0:T(8,128)} %fl_in.1, ...), custom_call_target="tpu_custom_call" | custom-call | tf_op jit(solution)/shard_map/pallas_call | solution.py:440
  36.5 0.7 %copy.11 = f32[2048,32]{0,1:T(8,128)} copy(f32[2048,32]{0,1:T(8,128)S(1)} %bitcast.6) | data formatting | bytes 524288

commit v6 on v5

--- a/solution.py
+++ b/solution.py
@@ -318,12 +318,12 @@
     ]
     for copy in hs_out:
         copy.start()
+    for t in range(2, leaves + 1):
+        own_products(t)
     z_forward(steps[5])
     z_forward(steps[6])
     x_forward(steps[5])
     x_forward(steps[6])
-    for t in range(2, leaves + 1):
-        own_products(t)
     relay(1)
     relay(2)
     for h in range(2):
@@ -378,6 +378,8 @@
         to_sibling(steps[m], across, 2)
     for copy in a_out:
         copy.wait_recv()
+    for copy in vectors_out + points_out + lists_out + hv_out + hs_out + a_out + x_out + z_out:
+        copy.wait_send()
     for i in range(leaves):
         w, e = i // half_leaves, i % half_leaves
         near = acc[i, r]
@@ -419,7 +421,7 @@
     for i in range(leaves):
         out[:, block_of(i)] = out[:, block_of(i)] + fars[i]
 
-    for copy in vectors_out + points_out + lists_out + hv_out + hs_out + a_out + x_out + c_out + z_out:
+    for copy in c_out:
         copy.wait_send()
 
 

time: 37.5 us -> 37.5 us (level)
  no operation moved by 1% of the time
where the time goes in v6:
time: 37.5 us; the launch traced here: 37.4 us
  Pallas kernels  36.7 us (98%)
  local copies, waits for them, and re-layouts  0.71 us (2%)
    pallas_call x1, Pallas kernels, local(): pl.pallas_call(functools.partial(kernel, (zdim, xdim, ydim)), out_shape=p...  36.7 us

profile of v6, /device:TPU:1, one launch (start us, length us, event | category | flops | bytes accessed | tf_op | source)
XLA Modules:
  0.0 37.4 jit_solution(6817344675629363884)
XLA Ops:
  0.0 36.7 %shard_map.91 = f32[32,2048]{1,0:T(8,128)S(1)} custom-call(bf16[784,2048]{1,0:T(8,128)(2,1)} %bitcast.7, bf16[32,2048]{1,0:T(8,128)(2,1)} %bitcast.11, f32[8,64,256]{2,1,0:T(8,128)} %bitcast.10, f32[64,64,64]{2,1,0:T(8,128)} %bitcast.8, f32[8,64,64]{2,1,0:T(8,128)} %tr.1, f32[32,64,64]{2,1,0:T(8,128)} %bitcast.9, s32[8,8]{1,0:T(8,128)} %fl_in.1, ...), custom_call_target="tpu_custom_call" | custom-call | tf_op jit(solution)/shard_map/pallas_call | solution.py:442
  36.7 0.7 %copy.11 = f32[2048,32]{0,1:T(8,128)} copy(f32[2048,32]{0,1:T(8,128)S(1)} %bitcast.6) | data formatting | bytes 524288
